TPU v7x, 32 devices: a whole 2x2x4 slice. The times are simulated.
32 devices in a mesh: section: 4 (over z), seq: 8 (over y, x, core).
Axes of the slice: x: 2, y: 2, z: 4, core: 2. Of those that a mesh axis runs over, the one named last changes fastest.
Arguments:
- input_in_transit: bfloat16 [4, 1024, 4096], P('section', 'seq'), may hold values from -6 to 6
- mixer_norm_gain: float32 [4, 4096], P('section'), may hold values from 0.5 to 1.5
- convolution_weight: float32 [4, 4, 4096], P('section'), may hold values from -3 to 3
- convolution_bias: float32 [4, 4096], P('section'), may hold values from -2 to 2
- input_projection: bfloat16 [4, 4096, 288], P('section', 'seq'), may hold values from -0.09375 to 0.09375
- step_size_projection: bfloat16 [4, 256, 4096], P('section', None, 'seq'), may hold values from -0.375 to 0.375
- step_size_bias: float32 [4, 4096], P('section'), may hold values from -6.9 to -2.3
- log_decay_rates: float32 [4, 4096, 16], P('section'), may hold values from 0 to 2.77
- mixer_skip_weight: float32 [4, 4096], P('section'), may hold values from 0.5 to 1.5
- expert_norm_gain: float32 [4, 4096], P('section'), may hold values from 0.1 to 1.9
- router: bfloat16 [4, 4096, 16], P('section'), may hold values from -0.09375 to 0.09375
- gate_weight: bfloat16 [4, 4096, 12288], P('section', None, 'seq'), may hold values from -0.09375 to 0.09375
- up_weight: bfloat16 [4, 4096, 12288], P('section', None, 'seq'), may hold values from -0.09375 to 0.09375
- down_weight: bfloat16 [4, 12288, 4096], P('section', 'seq'), may hold values from -0.0546875 to 0.0546875
- expert_index_table: int32 [2, 4, 1024, 2], P(None, 'section', 'seq'), may hold values from 0 to 15, as said below
Outputs:
- layer_out: bfloat16 [4, 1024, 4096], P('section', 'seq')
Inputs may be any that keep to these rules, and one draw needn't show every extreme that they name: `expert_index_table`: each token names two different experts of the 16; for each step and section, expert 0 is named by at most 8 tokens of any one block of 128 tokens.
All inputs are finite; a program needn't handle non-finite values.
Results may differ from a plain program's by a relative error of at most 0.0086.
Values may be sent and summed in bfloat16 or wider, within the bound.
A program may use at most 128 MiB of HBM per device.

v0:
```python
import functools

import jax
import jax.numpy as jnp
from jax import lax
from jax.experimental import pallas as pl
from jax.experimental.pallas import tpu as pltpu
from jax.sharding import PartitionSpec as P

STEPS = 2
LANES = 128
ROWS = 8
LOG2E = 1.4426950408889634
MESH = pl.DeviceIdType.MESH
SMALL_VMEM = 8 * 1024 * 1024


def greet(axis):
    n, me = lax.axis_size(axis), lax.axis_index(axis)
    barrier = pltpu.get_barrier_semaphore()
    for k in range(1, n):
        pl.semaphore_signal(
            barrier, inc=1, device_id={axis: lax.rem(me + k, n)}, device_id_type=MESH
        )
    pl.semaphore_wait(barrier, n - 1)


def exchange_kernel(axis, parts, *refs):
    n, me = lax.axis_size(axis), lax.axis_index(axis)
    count = len(parts)
    send_sem, recv_sem, local_sem = refs[2 * count :]
    greet(axis)
    copies = []
    for k in range(1, n):
        peer = lax.rem(me + k, n)
        for p, (src_at, dst_at) in enumerate(parts):
            copy = pltpu.make_async_remote_copy(
                src_ref=src_at(refs[p], peer),
                dst_ref=dst_at(refs[count + p], me),
                send_sem=send_sem.at[p, k],
                recv_sem=recv_sem.at[p, k],
                device_id={axis: peer},
                device_id_type=MESH,
            )
            copy.start()
            copies.append(copy)
    for p, (src_at, dst_at) in enumerate(parts):
        own = pltpu.make_async_copy(
            src_at(refs[p], me), dst_at(refs[count + p], me), local_sem.at[p]
        )
        own.start()
        copies.append(own)
    for copy in copies:
        copy.wait()


def exchange(xs, shapes, parts, axis, cid):
    n, count = lax.axis_size(axis), len(xs)
    return pl.pallas_call(
        functools.partial(exchange_kernel, axis, parts),
        out_shape=[jax.ShapeDtypeStruct(shape, x.dtype) for x, shape in zip(xs, shapes)],
        in_specs=[pl.BlockSpec(memory_space=pl.ANY)] * count,
        out_specs=[pl.BlockSpec(memory_space=pl.ANY)] * count,
        scratch_shapes=[
            pltpu.SemaphoreType.DMA((count, n)),
            pltpu.SemaphoreType.DMA((count, n)),
            pltpu.SemaphoreType.DMA((count,)),
        ],
        compiler_params=pltpu.CompilerParams(
            collective_id=cid, has_side_effects=True, vmem_limit_bytes=SMALL_VMEM
        ),
        name=f"exchange_{cid}",
    )(*xs)


def spread(axis, block, place, o_ref, send_sem, recv_sem, relay_send, relay_recv, local_sem):
    n, me = lax.axis_size(axis), lax.axis_index(axis)
    partner = me + 1 - 2 * lax.rem(me, 2)

    def send(source, at, target, sent, received):
        copy = pltpu.make_async_remote_copy(
            src_ref=source,
            dst_ref=place(o_ref, at),
            send_sem=sent,
            recv_sem=received,
            device_id={axis: target},
            device_id_type=MESH,
        )
        copy.start()
        return copy

    far = [
        send(block, me, lax.rem(me + 2 * k, n), send_sem.at[k], recv_sem.at[k])
        for k in range(1, n // 2)
    ]
    near = [send(block, me, partner, relay_send.at[0], relay_recv.at[0])]
    own = pltpu.make_async_copy(block, place(o_ref, me), local_sem)
    own.start()
    for k in range(1, n // 2):
        far[k - 1].wait_recv()
        source = lax.rem(me + n - 2 * k, n)
        near.append(
            send(place(o_ref, source), source, partner, relay_send.at[k], relay_recv.at[k])
        )
    for copy in far:
        copy.wait_send()
    for copy in near:
        copy.wait()
    own.wait()


def spread_scratch(n):
    return [pltpu.SemaphoreType.DMA((n // 2,))] * 4 + [pltpu.SemaphoreType.DMA]


def gather_kernel(axis, place, x_ref, o_ref, *sems):
    greet(axis)
    spread(axis, x_ref, place, o_ref, *sems)


def gather(x, shape, place, axis, cid):
    return pl.pallas_call(
        functools.partial(gather_kernel, axis, place),
        out_shape=jax.ShapeDtypeStruct(shape, x.dtype),
        in_specs=[pl.BlockSpec(memory_space=pl.ANY)],
        out_specs=pl.BlockSpec(memory_space=pl.ANY),
        scratch_shapes=spread_scratch(lax.axis_size(axis)),
        compiler_params=pltpu.CompilerParams(
            collective_id=cid, has_side_effects=True, vmem_limit_bytes=SMALL_VMEM
        ),
        name=f"gather_{cid}",
    )(x)


def reduce_here(axis, src_at, x_ref, held, send_sem, recv_sem, local_sem):
    n, me = lax.axis_size(axis), lax.axis_index(axis)
    copies = []
    for k in range(1, n):
        peer = lax.rem(me + k, n)
        copy = pltpu.make_async_remote_copy(
            src_ref=src_at(x_ref, peer),
            dst_ref=held.at[k],
            send_sem=send_sem.at[k],
            recv_sem=recv_sem.at[k],
            device_id={axis: peer},
            device_id_type=MESH,
        )
        copy.start()
        copies.append(copy)
    own = pltpu.make_async_copy(src_at(x_ref, me), held.at[0], local_sem)
    own.start()
    own.wait()
    total = held[0].astype(jnp.float32)
    for k in range(1, n):
        copies[k - 1].wait()
        total = total + held[k].astype(jnp.float32)
    return total


def reduce_scratch(n, shape, dtype):
    return [
        pltpu.VMEM((n,) + shape, dtype),
        pltpu.SemaphoreType.DMA((n,)),
        pltpu.SemaphoreType.DMA((n,)),
        pltpu.SemaphoreType.DMA,
    ]


def scatter_sum_kernel(axis, src_at, x_ref, o_ref, *scratch):
    greet(axis)
    o_ref[...] = reduce_here(axis, src_at, x_ref, *scratch)


def scatter_sum(x, shape, src_at, axis, cid):
    return pl.pallas_call(
        functools.partial(scatter_sum_kernel, axis, src_at),
        out_shape=jax.ShapeDtypeStruct(shape, jnp.float32),
        in_specs=[pl.BlockSpec(memory_space=pl.ANY)],
        out_specs=pl.BlockSpec(memory_space=pltpu.VMEM),
        scratch_shapes=reduce_scratch(lax.axis_size(axis), shape, x.dtype),
        compiler_params=pltpu.CompilerParams(
            collective_id=cid, has_side_effects=True, vmem_limit_bytes=SMALL_VMEM
        ),
        name=f"scatter_sum_{cid}",
    )(x)


def project_kernel(axis, src_at, place, rank, x_ref, o_ref, held, s1, s2, s3, stage, *sems):
    greet(axis)
    total = reduce_here(axis, src_at, x_ref, held, s1, s2, s3)
    end = total.shape[0]
    stage[:end, :] = total.astype(jnp.bfloat16)
    maps = total[rank:]
    stage[end:, :] = (maps - maps.astype(jnp.bfloat16).astype(jnp.float32)).astype(jnp.bfloat16)
    spread(axis, stage, place, o_ref, *sems)


def project(x, rank, block, axis, cid):
    n, (rows, length) = lax.axis_size(axis), x.shape
    tall = 2 * rows - rank
    return pl.pallas_call(
        functools.partial(project_kernel, axis, column_block(block), column_block(block), rank),
        out_shape=jax.ShapeDtypeStruct((tall, length), x.dtype),
        in_specs=[pl.BlockSpec(memory_space=pl.ANY)],
        out_specs=pl.BlockSpec(memory_space=pl.ANY),
        scratch_shapes=reduce_scratch(n, (rows, block), x.dtype)
        + [pltpu.VMEM((tall, block), x.dtype)]
        + spread_scratch(n),
        compiler_params=pltpu.CompilerParams(
            collective_id=cid, has_side_effects=True, vmem_limit_bytes=SMALL_VMEM
        ),
        name=f"project_{cid}",
    )(x)


def row_block(size):
    return lambda ref, i: ref.at[pl.ds(pl.multiple_of(i * size, size), size), :]


def column_block(size):
    return lambda ref, i: ref.at[:, pl.ds(pl.multiple_of(i * size, size), size)]


def whole(ref, i):
    return ref


def slot_of(ref, i):
    return ref.at[i]


def folded(parts):
    sub = lax.broadcasted_iota(jnp.int32, parts[0].shape, 0)
    reach = ROWS // 2
    while reach:
        low = (sub // reach) % 2 == 0
        half = len(parts) // 2
        merged = []
        for a, b in zip(parts[:half], parts[half:]):
            keep = jnp.where(low, a, b)
            give = jnp.where(low, b, a)
            if reach == ROWS // 2:
                moved = pltpu.roll(give, reach, 0)
            else:
                moved = jnp.where(
                    low, pltpu.roll(give, ROWS - reach, 0), pltpu.roll(give, reach, 0)
                )
            merged.append(keep + moved)
        parts = merged
        reach //= 2
    return parts[0]


def scan_kernel(nstate, dt_ref, x_ref, bc_ref, a_ref, o_ref, h_ref):
    @pl.when(pl.program_id(0) == 0)
    def _():
        h_ref[...] = jnp.zeros_like(h_ref)

    groups = nstate // ROWS
    chunk = dt_ref.shape[0]
    tile = (ROWS, dt_ref.shape[1])
    rates = [a_ref[g * ROWS : (g + 1) * ROWS, :] for g in range(groups)]

    def block(i, states):
        states = list(states)
        base = pl.multiple_of(i * ROWS, ROWS)
        bc = pltpu.roll(bc_ref[...], lax.rem(chunk - i * ROWS, chunk), 1)
        parts = []
        for k in range(ROWS):
            d = jnp.broadcast_to(dt_ref[pl.ds(base + k, 1), :], tile)
            v = d * jnp.broadcast_to(x_ref[pl.ds(base + k, 1), :], tile)
            total = None
            for g in range(groups):
                b = bc[g * ROWS : (g + 1) * ROWS, k : k + 1]
                c = bc[nstate + g * ROWS : nstate + (g + 1) * ROWS, k : k + 1]
                states[g] = jnp.exp2(d * rates[g]) * states[g] + v * b
                term = states[g] * c
                total = term if total is None else total + term
            parts.append(total)
        o_ref[pl.ds(base, ROWS), :] = folded(parts)
        return tuple(states)

    states = tuple(h_ref[g * ROWS : (g + 1) * ROWS, :] for g in range(groups))
    states = lax.fori_loop(0, chunk // ROWS, block, states)
    for g in range(groups):
        h_ref[g * ROWS : (g + 1) * ROWS, :] = states[g]


def selective_scan(dt, x, bc, rates):
    length, width = dt.shape
    nstate = rates.shape[0]
    chunk = LANES
    return pl.pallas_call(
        functools.partial(scan_kernel, nstate),
        out_shape=jax.ShapeDtypeStruct((length, width), jnp.float32),
        grid=(length // chunk,),
        in_specs=[
            pl.BlockSpec((chunk, width), lambda i: (i, 0)),
            pl.BlockSpec((chunk, width), lambda i: (i, 0)),
            pl.BlockSpec((2 * nstate, chunk), lambda i: (0, i)),
            pl.BlockSpec((nstate, width), lambda i: (0, 0)),
        ],
        out_specs=pl.BlockSpec((chunk, width), lambda i: (i, 0)),
        scratch_shapes=[pltpu.VMEM((nstate, width), jnp.float32)],
        compiler_params=pltpu.CompilerParams(vmem_limit_bytes=SMALL_VMEM),
        cost_estimate=pl.CostEstimate(
            flops=6 * length * width * nstate,
            bytes_accessed=12 * length * width,
            transcendentals=length * width * nstate,
        ),
        name="selective_scan",
    )(dt, x, bc, rates)


def passed_along(x, axis):
    length = lax.axis_size(axis)
    return lax.ppermute(x, axis, [(i, (i + 1) % length) for i in range(length)])


def dispatch_of(ids, blocks, capacity):
    length = ids.shape[0]
    size = length // blocks
    routed = (ids[:, 0] == 0) | (ids[:, 1] == 0)
    counted = routed.astype(jnp.float32).reshape(blocks, size)
    before = jnp.tril(jnp.ones((size, size), jnp.float32), -1)
    rank = jnp.dot(counted, before.T).reshape(length)
    slot = rank.astype(jnp.int32) + (jnp.arange(length, dtype=jnp.int32) // size) * capacity
    chosen = (jnp.arange(blocks * capacity, dtype=jnp.int32)[:, None] == slot[None, :]) & routed[
        None, :
    ]
    return chosen.astype(jnp.bfloat16), routed


def body(
    input_in_transit,
    mixer_norm_gain,
    convolution_weight,
    convolution_bias,
    input_projection,
    step_size_projection,
    step_size_bias,
    log_decay_rates,
    mixer_skip_weight,
    expert_norm_gain,
    router,
    gate_weight,
    up_weight,
    down_weight,
    expert_index_table,
):
    n, me = lax.axis_size("seq"), lax.axis_index("seq")
    experts = router.shape[2]
    rows = input_in_transit.shape[1]
    model = input_in_transit.shape[2]
    nstate = log_decay_rates.shape[2]
    rank = step_size_projection.shape[1]
    kernel = convolution_weight.shape[1]
    capacity = rows // 16
    length, width = rows * n, model // n
    slots = capacity * n
    f32, bf16 = jnp.float32, jnp.bfloat16

    def own(weight, axis):
        return lax.dynamic_slice_in_dim(weight, me * width, width, axis)

    gain = own(mixer_norm_gain[0], 0)
    taps = own(convolution_weight[0], 1)
    conv_bias = own(convolution_bias[0], 0)
    dt_bias = own(step_size_bias[0], 0)
    rates = -LOG2E * jnp.exp(own(log_decay_rates[0], 0)).T
    skip = own(mixer_skip_weight[0], 0)
    columns = rank + 2 * nstate

    tokens = input_in_transit[0]
    as_float = tokens.astype(f32)
    square = jnp.sum(as_float * as_float, axis=-1)
    ids = expert_index_table[:, 0].astype(f32)
    small = jnp.concatenate(
        [ids.transpose(0, 2, 1).reshape(2 * STEPS, rows), square[None]], 0
    )
    small = jnp.pad(small, ((0, -small.shape[0] % ROWS), (0, 0)))
    small, present = exchange(
        [small, tokens],
        [(n,) + small.shape, (length, width)],
        [(whole, slot_of), (column_block(width), row_block(rows))],
        "seq",
        1,
    )
    square = small[:, 2 * STEPS].reshape(length)
    all_ids = small[:, : 2 * STEPS].reshape(n, STEPS, 2, rows).transpose(1, 0, 3, 2)
    all_ids = all_ids.reshape(STEPS, length, 2)
    for step in range(STEPS):
        if step:
            as_float = present.astype(f32)
            part = jnp.sum(as_float * as_float, axis=-1).reshape(n, rows)
            part = jnp.pad(part, ((0, -n % ROWS), (0, 0)))
            (part,) = exchange([part], [(n,) + part.shape], [(whole, slot_of)], "seq", 3)
            square = jnp.sum(part, axis=0)[:n].reshape(length)
        scale = lax.rsqrt(square / model + 1e-06)
        normed = (present.astype(f32) * scale[:, None] * gain).astype(bf16)
        padded = jnp.concatenate([jnp.zeros((kernel - 1, width), bf16), normed], 0)
        convolved = conv_bias
        for tap in range(kernel):
            convolved = convolved + taps[tap] * padded[tap : tap + length].astype(f32)
        inner = jax.nn.silu(convolved)
        partial = lax.dot_general(
            input_projection[0],
            inner.astype(bf16),
            (((0,), (1,)), ((), ())),
            preferred_element_type=f32,
        ).astype(bf16)
        everyone = project(partial, rank, rows, "seq", 4)
        bc = everyone[rank:columns].astype(f32) + everyone[columns:].astype(f32)
        step_size = jax.nn.softplus(
            lax.dot_general(
                everyone[:rank],
                step_size_projection[0],
                (((0,), (0,)), ((), ())),
                preferred_element_type=f32,
            )
            + dt_bias
        )
        scanned = selective_scan(step_size, inner, bc, rates)
        mixed = (present.astype(f32) + (scanned + skip * inner)).astype(bf16)
        dispatch, routed = dispatch_of(all_ids[step], n, capacity)
        picked = jnp.dot(dispatch, mixed, preferred_element_type=f32).astype(bf16)
        last = step + 1 == STEPS
        if not last:
            moved = passed_along(mixed, "section")
            moved_ids = passed_along(all_ids[step], "section")
        full = gather(picked, (slots, model), column_block(width), "seq", 6)
        if last:
            mixed = lax.all_to_all(
                mixed.reshape(n, rows, width), "seq", split_axis=0, concat_axis=0
            )
            mixed = mixed.transpose(1, 0, 2).reshape(rows, model)
        full_float = full.astype(f32)
        moe_in = (
            full_float
            * lax.rsqrt(jnp.mean(full_float * full_float, axis=-1, keepdims=True) + 1e-06)
            * expert_norm_gain[0]
        ).astype(bf16)
        logits = jnp.dot(moe_in, router[0], preferred_element_type=f32)
        slot_ids = jnp.dot(dispatch, all_ids[step].astype(bf16), preferred_element_type=f32)
        one_hot = (
            slot_ids[:, :, None] == jnp.arange(experts, dtype=jnp.int32).astype(f32)
        ).astype(f32)
        first = jnp.sum(logits * one_hot[:, 0], axis=1)
        second = jnp.sum(logits * one_hot[:, 1], axis=1)
        weight_one = jax.nn.sigmoid(first - second)
        route = jnp.where(
            slot_ids[:, 0] == 0,
            weight_one,
            jnp.where(slot_ids[:, 1] == 0, 1.0 - weight_one, jnp.zeros_like(weight_one)),
        )
        gate_part = jnp.dot(moe_in, gate_weight[0], preferred_element_type=f32)
        up_part = jnp.dot(moe_in, up_weight[0], preferred_element_type=f32)
        hidden = (jax.nn.silu(gate_part) * up_part).astype(bf16)
        terms = jnp.dot(hidden, down_weight[0], preferred_element_type=f32).astype(bf16)
        if last:
            terms = terms.reshape(n, capacity, model)
            expert_out = scatter_sum(terms, (capacity, model), slot_of, "seq", 8)
            dispatch = lax.dynamic_slice(
                dispatch, (me * capacity, me * rows), (capacity, rows)
            )
            routed = lax.dynamic_slice_in_dim(routed, me * rows, rows, 0)
            route = lax.dynamic_slice_in_dim(route, me * capacity, capacity, 0)
            picked = lax.dynamic_slice_in_dim(full, me * capacity, capacity, 0)
        else:
            expert_out = scatter_sum(terms, (slots, width), column_block(width), "seq", 7)
        expert_out = expert_out.astype(bf16).astype(f32)
        new_rows = (picked.astype(f32) + route[:, None] * expert_out).astype(bf16)
        if not last:
            new_rows = passed_along(new_rows, "section")
            dispatch, routed = dispatch_of(moved_ids, n, capacity)
            mixed = moved
        placed = lax.dot_general(
            dispatch, new_rows, (((0,), (0,)), ((), ())), preferred_element_type=f32
        ).astype(bf16)
        present = jnp.where(routed[:, None], placed, mixed)
    return present[None]


def solution(mesh):
    return jax.shard_map(
        body,
        mesh=mesh,
        in_specs=(
            P("section", "seq", None),
            P("section", None),
            P("section", None, None),
            P("section", None),
            P("section", "seq", None),
            P("section", None, "seq"),
            P("section", None),
            P("section", None, None),
            P("section", None),
            P("section", None),
            P("section", None, None),
            P("section", None, "seq"),
            P("section", None, "seq"),
            P("section", "seq", None),
            P(None, "section", "seq", None),
        ),
        out_specs=P("section", "seq", None),
        check_vma=False,
    )
```

profile of v0, /device:TPU:1, one launch (start us, length us, event | category | flops | bytes accessed | tf_op | source)
XLA Modules:
  0.0 211.9 jit_solution(1987386147563754772)
XLA Ops:
  0.0 0.7 convert_element_type.202
  0.7 1.5 multiply_reduce_fusion
  2.3 1.2 copy-done.2
  3.5 16.7 %exchange_1.1 = (f32[8,8,128]{2,1,0:T(8,128)S(1)}, bf16[1024,512]{1,0:T(8,128)(2,1)S(1)}) custom-call(f32[8,128]{1,0:T(8,128)S(1)} %select_maximum_fusion.refs_0_, bf16[128,4096]{1,0:T(8,128)(2,1)S(1)} %bitcast.165), custom_call_target="tpu_custom_call" | custom-call | tf_op jit(solution)/shard_map/exchange_1/pallas_call | solution.py:59
  20.2 0.7 constant_dynamic-slice_fusion.3
  20.9 0.7 constant_dynamic-slice_fusion.4
  21.6 0.3 fusion.36
  22.0 0.9 constant_dynamic-slice_fusion.2
  22.9 1.4 divide_multiply_fusion.1.x_ref
  24.3 0.0 copy-start.4
  24.3 0.5 fusion.42.x_ref
  24.8 16.8 %project_4.2 = bf16[320,1024]{1,0:T(8,128)(2,1)S(1)} custom-call(bf16[288,1024]{1,0:T(8,128)(2,1)S(1)} %fusion.42.x_ref), custom_call_target="tpu_custom_call" | custom-call | tf_op jit(solution)/shard_map/project_4/pallas_call | solution.py:201
  41.7 0.8 multiply_bitcast_fusion.a_ref
  42.5 1.4 compare_select_fusion.1.dt_ref
  43.8 0.0 slice-start
  43.8 0.0 slice-start.1
  43.9 26.6 %selective_scan.2 = f32[1024,512]{1,0:T(8,128)S(1)} custom-call(f32[1024,512]{1,0:T(8,128)S(1)} %compare_select_fusion.1.dt_ref, f32[1024,512]{1,0:T(8,128)S(1)} %divide_multiply_fusion.1.x_ref, f32[32,1024]{1,0:T(8,128)S(1)} %convert_add_fusion.3.bc_ref, f32[16,512]{1,0:T(8,128)S(1)} %multiply_bitcast_fusion.a_ref), custom_call_target="tpu_custom_call" | custom-call | flops 50331648 | bytes 6291456 | tf_op jit(solution)/shard_map/selective_scan/pallas_call | solution.py:293
  70.4 0.0 slice-start.2
  70.4 1.7 fusion.37
  72.1 0.0 copy-start.3
  72.1 1.3 collective-permute-start.2
  73.5 1.5 collective-permute-start
  75.1 0.2 fusion.49
  75.3 0.3 convolution_convert_fusion.5.x_ref
  75.6 0.2 fusion.84
  75.8 8.4 %gather_6.2 = bf16[64,4096]{1,0:T(8,128)(2,1)S(1)} custom-call(bf16[64,512]{1,0:T(8,128)(2,1)S(1)} %convolution_convert_fusion.5.x_ref), custom_call_target="tpu_custom_call" | custom-call | tf_op jit(solution)/shard_map/gather_6/pallas_call | solution.py:122
  84.2 0.2 fusion.50
  84.5 0.2 fusion.47
  84.7 0.2 fusion.125
  84.9 0.0 slice-done.2
  84.9 2.4 %fusion.10 = f32[64,1536]{1,0:T(8,128)S(1)} fusion(bf16[1,4096,1536]{2,1,0:T(8,128)(2,1)S(1)} %bitcast.168, bf16[64,4096]{1,0:T(8,128)(2,1)S(1)} %gather_6.2, f32[4096]{0:T(1024)S(1)} %bitcast.173, f32[64]{0:T(128)S(1)} %add_rsqrt_fusion.2), kind=kOutput, calls=%fused_computation.10 | convolution fusion | flops 806354944 | bytes 13517056 | tf_op jit(solution)/shard_map/dot_general | solution.py:456
  87.2 0.0 copy-start.5
  87.3 12.8 %fusion.14.x_ref = bf16[64,4096]{1,0:T(8,128)(2,1)S(1)} fusion(bf16[1,1536,4096]{2,1,0:T(8,128)(2,1)} %param.28, bf16[1,4096,1536]{2,1,0:T(8,128)(2,1)} %param.27, f32[64,1536]{1,0:T(8,128)S(1)} %fusion.10, bf16[64,4096]{1,0:T(8,128)(2,1)S(1)} %gather_6.2, f32[4096]{0:T(1024)S(1)} %bitcast.174, f32[64]{0:T(128)S(1)} %add_rsqrt_fusion.2), kind=kOutput, calls=%fused_computation.17 | convolution fusion | flops 1612513280 | bytes 26624256 | tf_op jit(solution)/shard_map/dot_general | solution.py:459
  100.0 9.1 %scatter_sum_7.1 = f32[64,512]{1,0:T(8,128)S(1)} custom-call(bf16[64,4096]{1,0:T(8,128)(2,1)S(1)} %fusion.14.x_ref), custom_call_target="tpu_custom_call" | custom-call | tf_op jit(solution)/shard_map/scatter_sum_7/pallas_call | solution.py:175
  109.1 0.1 compare_convert_fusion
  109.2 0.3 fusion.119
  109.6 0.1 add_convert_fusion.1
  109.7 1.6 collective-permute-start.1
  111.3 0.0 collective-permute-done
  111.3 0.2 fusion.48
  111.5 4.2 %collective-permute-done.1 = bf16[64,512]{1,0:T(8,128)(2,1)S(1)} collective-permute-done((bf16[64,512]{1,0:T(8,128)(2,1)S(1)}, bf16[64,512]{1,0:T(8,128)(2,1)S(1)}, u32[]{:S(2)}, u32[]{:S(2)}) %collective-permute-start.1) | collective-permute-done | bytes 65568 | tf_op jit(solution)/shard_map/ppermute | solution.py:317
  115.8 0.0 collective-permute-done.2
  115.8 1.9 fusion.38
  117.7 4.8 %exchange_3.1 = f32[8,8,128]{2,1,0:T(8,128)S(1)} custom-call(f32[8,128]{1,0:T(8,128)S(1)} %bitcast.166), custom_call_target="tpu_custom_call" | custom-call | tf_op jit(solution)/shard_map/exchange_3/pallas_call | solution.py:59
  122.6 0.3 fusion.40
  122.9 1.4 divide_multiply_fusion.x_ref
  124.2 0.5 fusion.43.x_ref
  124.8 17.1 %project_4.3 = bf16[320,1024]{1,0:T(8,128)(2,1)S(1)} custom-call(bf16[288,1024]{1,0:T(8,128)(2,1)S(1)} %fusion.43.x_ref), custom_call_target="tpu_custom_call" | custom-call | tf_op jit(solution)/shard_map/project_4/pallas_call | solution.py:201
  141.9 0.0 slice-start.3
  141.9 1.4 compare_select_fusion.dt_ref
  143.3 0.0 slice-start.4
  143.3 26.6 %selective_scan.3 = f32[1024,512]{1,0:T(8,128)S(1)} custom-call(f32[1024,512]{1,0:T(8,128)S(1)} %compare_select_fusion.dt_ref, f32[1024,512]{1,0:T(8,128)S(1)} %divide_multiply_fusion.x_ref, f32[32,1024]{1,0:T(8,128)S(1)} %convert_add_fusion.2.bc_ref, f32[16,512]{1,0:T(8,128)S(1)} %multiply_bitcast_fusion.a_ref), custom_call_target="tpu_custom_call" | custom-call | flops 50331648 | bytes 6291456 | tf_op jit(solution)/shard_map/selective_scan/pallas_call | solution.py:293
  169.9 2.6 %fusion.41 = bf16[1024,512]{1,0:T(8,128)(2,1)} fusion(bf16[1024,512]{1,0:T(8,128)(2,1)S(1)} %get-tuple-element.24, f32[1024,512]{1,0:T(8,128)S(1)} %selective_scan.3, f32[512]{0:T(512)S(1)} %bitcast.203, bf16[1024,512]{1,0:T(8,128)(2,1)S(1)} %fusion.40, f32[512]{0:T(512)S(1)} %bitcast.201, f32[512]{0:T(512)S(1)} %bitcast.193, f32[512]{0:T(512)S(1)} %bitcast.197, ...), kind=kLoop, calls=%fused_computation.35 | loop fusion | flops 11010048 | bytes 5255168 | tf_op jit(solution)/shard_map/convert_element_type | solution.py:424
  172.6 1.5 convolution_convert_fusion.4.x_ref
  174.1 7.2 %gather_6.3 = bf16[64,4096]{1,0:T(8,128)(2,1)S(1)} custom-call(bf16[64,512]{1,0:T(8,128)(2,1)S(1)} %convolution_convert_fusion.4.x_ref), custom_call_target="tpu_custom_call" | custom-call | tf_op jit(solution)/shard_map/gather_6/pallas_call | solution.py:122
  181.2 0.2 fusion.53
  181.5 2.4 %fusion.8 = f32[64,1536]{1,0:T(8,128)S(1)} fusion(bf16[1,4096,1536]{2,1,0:T(8,128)(2,1)S(1)} %bitcast.170, bf16[64,4096]{1,0:T(8,128)(2,1)S(1)} %gather_6.3, f32[64]{0:T(128)S(1)} %add_rsqrt_fusion.1, f32[4096]{0:T(1024)S(1)} %bitcast.176), kind=kOutput, calls=%fused_computation.8 | convolution fusion | flops 806354944 | bytes 13517056 | tf_op jit(solution)/shard_map/dot_general | solution.py:456
  183.8 3.8 %all-to-all-start = ((bf16[8,128,512]{2,1,0:T(8,128)(2,1)}), bf16[8,128,512]{2,1,0:T(8,128)(2,1)S(1)}, u32[]{:S(2)}, u32[]{:S(2)}) async-start(bf16[8,128,512]{2,1,0:T(8,128)(2,1)} %bitcast.46), calls=%async_computation | async-start | bytes 2097152 | tf_op jit(solution)/shard_map/all_to_all | solution.py:433
  187.6 12.7 %fusion.20.x_ref = bf16[8,8,4096]{2,1,0:T(8,128)(2,1)S(1)} fusion(bf16[1,1536,4096]{2,1,0:T(8,128)(2,1)} %param.28, bf16[1,4096,1536]{2,1,0:T(8,128)(2,1)} %param.27, f32[64,1536]{1,0:T(8,128)S(1)} %fusion.8, bf16[64,4096]{1,0:T(8,128)(2,1)S(1)} %gather_6.3, f32[64]{0:T(128)S(1)} %add_rsqrt_fusion.1, f32[4096]{0:T(1024)S(1)} %bitcast.177), kind=kOutput, calls=%fused_computation.19 | convolution fusion | flops 1612513280 | bytes 26624256 | tf_op jit(solution)/shard_map/dot_general | solution.py:459
  200.3 9.5 %scatter_sum_8.1 = f32[8,4096]{1,0:T(8,128)S(1)} custom-call(bf16[8,8,4096]{2,1,0:T(8,128)(2,1)S(1)} %fusion.20.x_ref), custom_call_target="tpu_custom_call" | custom-call | tf_op jit(solution)/shard_map/scatter_sum_8/pallas_call | solution.py:175
  209.8 0.3 fusion.115
  210.2 0.1 dynamic_slice.42
  210.3 0.1 copy.17
  210.4 1.5 fusion.13
  (36 shorter events, 0.3 us)
Async XLA Ops:
  0.0 24.3 %copy-start = (bf16[1,512,288]{1,2,0:T(8,128)(2,1)S(1)}, bf16[1,512,288]{1,2,0:T(8,128)(2,1)}, u32[]{:S(2)}) copy-start(bf16[1,512,288]{1,2,0:T(8,128)(2,1)} %param.19) | copy-start | bytes 884740
  2.3 1.2 copy-start.2
  24.3 18.2 %copy-start.4 = (bf16[1,256,512]{2,1,0:T(8,128)(2,1)S(1)}, bf16[1,256,512]{2,1,0:T(8,128)(2,1)}, u32[]{:S(2)}) copy-start(bf16[1,256,512]{2,1,0:T(8,128)(2,1)} %param.20) | copy-start | bytes 786436
  43.8 41.0 %slice-start = ((s8[12582912]{0:T(1024)(128)(4,1)}), s8[4194304]{0:T(1024)(128)(4,1)S(1)}, s32[]{:S(2)}) async-start(s8[12582912]{0:T(1024)(128)(4,1)} %bitcast.167), calls=%async_computation.1 | async-start | bytes 8388608
  43.8 41.0 %slice-start.1 = ((s8[12582912]{0:T(1024)(128)(4,1)}), s8[4194304]{0:T(1024)(128)(4,1)S(1)}, s32[]{:S(2)}) async-start(s8[12582912]{0:T(1024)(128)(4,1)} %bitcast.167), calls=%async_computation.2 | async-start | bytes 8388608
  70.4 14.4 %slice-start.2 = ((s8[12582912]{0:T(1024)(128)(4,1)}), s8[4194304]{0:T(1024)(128)(4,1)S(1)}, s32[]{:S(2)}) async-start(s8[12582912]{0:T(1024)(128)(4,1)} %bitcast.167), calls=%async_computation.3 | async-start | bytes 8388608
  72.1 12.7 %copy-start.3 = (f32[1,4096]{1,0:T(1,128)S(1)}, f32[1,4096]{1,0:T(1,128)}, u32[]{:S(2)}) copy-start(f32[1,4096]{1,0:T(1,128)} %param.24) | copy-start | bytes 49156
  72.1 43.6 %collective-permute-start.2 = (bf16[1024,512]{1,0:T(8,128)(2,1)S(1)}, bf16[1024,512]{1,0:T(8,128)(2,1)}, u32[]{:S(2)}, u32[]{:S(2)}) collective-permute-start(bf16[1024,512]{1,0:T(8,128)(2,1)S(1)} %fusion.37), channel_id=1, source_target_pairs={{0,8},{8,16},{16,24},{24,0},{1,9},{9,17},{17,25},{25,1},{2,10},{10... | collective-permute-start | bytes 3145736 | tf_op jit(solution)/shard_map/ppermute | solution.py:317
  73.5 37.8 %collective-permute-start = (f32[1024,2]{0,1:T(2,128)S(1)}, f32[1024,2]{0,1:T(2,128)S(1)}, u32[]{:S(2)}, u32[]{:S(2)}) collective-permute-start(f32[1024,2]{0,1:T(2,128)S(1)} %get-tuple-element.20), channel_id=1, source_target_pairs={{0,8},{8,16},{16,24},{24,0},{1,9},{9,17},{17,25},{25,1},{2,10},{10... | collective-permute-start | bytes 24584 | tf_op jit(solution)/shard_map/ppermute | solution.py:317
  87.2 22.0 %copy-start.5 = (bf16[1,4096,16]{1,2,0:T(8,128)(2,1)S(1)}, bf16[1,4096,16]{1,2,0:T(8,128)(2,1)}, u32[]{:S(2)}) copy-start(bf16[1,4096,16]{1,2,0:T(8,128)(2,1)} %param.25) | copy-start | bytes 393220
  109.7 6.1 %collective-permute-start.1 = (bf16[64,512]{1,0:T(8,128)(2,1)S(1)}, bf16[64,512]{1,0:T(8,128)(2,1)S(1)}, u32[]{:S(2)}, u32[]{:S(2)}) collective-permute-start(bf16[64,512]{1,0:T(8,128)(2,1)S(1)} %add_convert_fusion.1), channel_id=1, source_target_pairs={{0,8},{8,16},{16,24},{24,0},{1,9},{9,17},{17,25},{25,1},{2,10},{10... | collective-permute-start | bytes 196616 | tf_op jit(solution)/shard_map/ppermute | solution.py:317
  141.9 39.5 %slice-start.3 = ((s8[12582912]{0:T(1024)(128)(4,1)}), s8[4194304]{0:T(1024)(128)(4,1)S(1)}, s32[]{:S(2)}) async-start(s8[12582912]{0:T(1024)(128)(4,1)} %bitcast.169), calls=%async_computation.4 | async-start | bytes 8388608
  143.3 38.1 %slice-start.4 = ((s8[12582912]{0:T(1024)(128)(4,1)}), s8[4194304]{0:T(1024)(128)(4,1)S(1)}, s32[]{:S(2)}) async-start(s8[12582912]{0:T(1024)(128)(4,1)} %bitcast.169), calls=%async_computation.5 | async-start | bytes 8388608
  143.3 38.1 %slice-start.5 = ((s8[12582912]{0:T(1024)(128)(4,1)}), s8[4194304]{0:T(1024)(128)(4,1)S(1)}, s32[]{:S(2)}) async-start(s8[12582912]{0:T(1024)(128)(4,1)} %bitcast.169), calls=%async_computation.6 | async-start | bytes 8388608
  183.8 26.5 %all-to-all-start = ((bf16[8,128,512]{2,1,0:T(8,128)(2,1)}), bf16[8,128,512]{2,1,0:T(8,128)(2,1)S(1)}, u32[]{:S(2)}, u32[]{:S(2)}) async-start(bf16[8,128,512]{2,1,0:T(8,128)(2,1)} %bitcast.46), calls=%async_computation | async-start | bytes 2097152 | tf_op jit(solution)/shard_map/all_to_all | solution.py:433
  210.3 1.6 copy-start.1
where the time goes:
time: 212 us
  Pallas kernels  143 us (67%)
  matrix products  40.7 us (19%)
  other arithmetic  11.6 us (5%)
  starting transfers between devices  8.24 us (4%)
  waiting for transfers between devices  4.23 us (2%)
  local copies, waits for them, and re-layouts  3.85 us (2%)
    pallas_call x2, Pallas kernels, selective_scan(): pl.pallas_call(functools.partial(scan_kernel, nstate), out_shape=jax.Shap...  53.1 us
    pallas_call x2, Pallas kernels, project(): pl.pallas_call(functools.partial(project_kernel, axis, column_block(block...  34 us
    dot_general x2, matrix products, body(): jnp.dot(hidden, down_weight[0], preferred_element_type=f32).astype(bf16)  25.5 us
    pallas_call x2, Pallas kernels, exchange(): pl.pallas_call(functools.partial(exchange_kernel, axis, parts), out_shape...  21.5 us
    pallas_call x2, Pallas kernels, scatter_sum(): pl.pallas_call(functools.partial(scatter_sum_kernel, axis, src_at), out_s...  18.6 us
    pallas_call x2, Pallas kernels, gather(): pl.pallas_call(functools.partial(gather_kernel, axis, place), out_shape=j...  15.6 us
    dot_general x2, matrix products, body(): gate_part = jnp.dot(moe_in, gate_weight[0], preferred_element_type=f32)  4.71 us
    ppermute x3, starting transfers between devices, passed_along(): return lax.ppermute(x, axis, [(i, (i + 1) % length) for i in range(length)])  4.46 us
  transfers between devices with their start and end apart: 4, of which 1 were waited for; matrix products, arithmetic and copies ran while one was open for 14% of the time, Pallas kernels for 13%

commit v1 on v0

--- a/solution.py
+++ b/solution.py
@@ -13,6 +13,9 @@
 LOG2E = 1.4426950408889634
 MESH = pl.DeviceIdType.MESH
 SMALL_VMEM = 8 * 1024 * 1024
+MIX_VMEM = 24 * 1024 * 1024
+PIECE = 16
+AHEAD = 2
 
 
 def greet(axis):
@@ -185,34 +188,6 @@
     )(x)
 
 
-def project_kernel(axis, src_at, place, rank, x_ref, o_ref, held, s1, s2, s3, stage, *sems):
-    greet(axis)
-    total = reduce_here(axis, src_at, x_ref, held, s1, s2, s3)
-    end = total.shape[0]
-    stage[:end, :] = total.astype(jnp.bfloat16)
-    maps = total[rank:]
-    stage[end:, :] = (maps - maps.astype(jnp.bfloat16).astype(jnp.float32)).astype(jnp.bfloat16)
-    spread(axis, stage, place, o_ref, *sems)
-
-
-def project(x, rank, block, axis, cid):
-    n, (rows, length) = lax.axis_size(axis), x.shape
-    tall = 2 * rows - rank
-    return pl.pallas_call(
-        functools.partial(project_kernel, axis, column_block(block), column_block(block), rank),
-        out_shape=jax.ShapeDtypeStruct((tall, length), x.dtype),
-        in_specs=[pl.BlockSpec(memory_space=pl.ANY)],
-        out_specs=pl.BlockSpec(memory_space=pl.ANY),
-        scratch_shapes=reduce_scratch(n, (rows, block), x.dtype)
-        + [pltpu.VMEM((tall, block), x.dtype)]
-        + spread_scratch(n),
-        compiler_params=pltpu.CompilerParams(
-            collective_id=cid, has_side_effects=True, vmem_limit_bytes=SMALL_VMEM
-        ),
-        name=f"project_{cid}",
-    )(x)
-
-
 def row_block(size):
     return lambda ref, i: ref.at[pl.ds(pl.multiple_of(i * size, size), size), :]
 
@@ -229,87 +204,228 @@
     return ref.at[i]
 
 
-def folded(parts):
-    sub = lax.broadcasted_iota(jnp.int32, parts[0].shape, 0)
-    reach = ROWS // 2
-    while reach:
-        low = (sub // reach) % 2 == 0
-        half = len(parts) // 2
-        merged = []
-        for a, b in zip(parts[:half], parts[half:]):
-            keep = jnp.where(low, a, b)
-            give = jnp.where(low, b, a)
-            if reach == ROWS // 2:
-                moved = pltpu.roll(give, reach, 0)
-            else:
-                moved = jnp.where(
-                    low, pltpu.roll(give, ROWS - reach, 0), pltpu.roll(give, reach, 0)
-                )
-            merged.append(keep + moved)
-        parts = merged
-        reach //= 2
-    return parts[0]
-
-
-def scan_kernel(nstate, dt_ref, x_ref, bc_ref, a_ref, o_ref, h_ref):
-    @pl.when(pl.program_id(0) == 0)
+def mixer_kernel(
+    axis, nstate, low_ref, maps_ref, x_ref, p_ref, w_ref, bias_ref, a_ref, skip_ref, o_ref,
+    full, bc, rs_low, rs_maps, dtb, vb, bb, cx, hb, yb, h_ref, ls, lr, ms, mr, gs, gr, bs, br,
+):
+    n, me = lax.axis_size(axis), lax.axis_index(axis)
+    f32, bf16 = jnp.float32, jnp.bfloat16
+    length, width = x_ref.shape
+    span = PIECE * n
+    blocks = length // span
+    groups = nstate // ROWS
+    wide = 2 * ROWS * nstate
+
+    def to(peer, source, target, sent, received):
+        return pltpu.make_async_remote_copy(
+            src_ref=source,
+            dst_ref=target,
+            send_sem=sent,
+            recv_sem=received,
+            device_id={axis: peer},
+            device_id_type=MESH,
+        )
+
+    def rows_of(j, device):
+        return pl.ds(pl.multiple_of(j * span + device * PIECE, PIECE), PIECE)
+
+    def lanes_of(j):
+        return pl.ds(pl.multiple_of(j * span, span), span)
+
+    def part_low(j, k):
+        peer = lax.rem(me + k, n)
+        return to(peer, low_ref.at[rows_of(j, peer), :], rs_low.at[j, k], ls.at[j, k], lr.at[j, k])
+
+    def part_maps(j, sender):
+        return to(j, maps_ref.at[:, lanes_of(j)], rs_maps.at[sender], ms.at[j], mr.at[sender])
+
+    def sum_low(j, k):
+        peer = lax.rem(me + k, n)
+        mine = full.at[rows_of(j, me), :]
+        return to(peer, mine, mine, gs.at[j, k], gr.at[j, k])
+
+    def sum_maps(j, k):
+        mine = bc.at[:, lanes_of(j)]
+        return to(lax.rem(me + k, n), mine, mine, bs.at[k], br.at[j])
+
+    def send_parts(j):
+        @pl.when(me != j)
+        def _():
+            part_maps(j, me).start()
+
+        for k in range(1, n):
+            part_low(j, k).start()
+
+    def reduce_and_send(j):
+        total = low_ref[rows_of(j, me), :].astype(f32)
+        for k in range(1, n):
+            part_low(j, k).wait_recv()
+            total = total + rs_low[j, k].astype(f32)
+        full[rows_of(j, me), :] = total.astype(bf16)
+        for k in range(1, n):
+            sum_low(j, k).start()
+
+        @pl.when(me == j)
+        def _():
+            maps = maps_ref[:, lanes_of(j)].astype(f32)
+            for k in range(1, n):
+                sender = lax.rem(me + k, n)
+                part_maps(j, sender).wait_recv()
+                maps = maps + rs_maps[sender].astype(f32)
+            high = maps.astype(bf16)
+            bc[: 2 * nstate, lanes_of(j)] = high
+            bc[2 * nstate :, lanes_of(j)] = (maps - high.astype(f32)).astype(bf16)
+            for k in range(1, n):
+                sum_maps(j, k).start()
+
+    spread_map = (
+        lax.broadcasted_iota(jnp.int32, (nstate, wide), 1) % nstate
+        == lax.broadcasted_iota(jnp.int32, (nstate, wide), 0)
+    ).astype(bf16)
+    own = (
+        lax.broadcasted_iota(jnp.int32, (LANES, wide), 1) // nstate
+        == lax.broadcasted_iota(jnp.int32, (LANES, wide), 0) % (2 * ROWS)
+    )
+
+    def chunk(start):
+        here = pl.ds(pl.multiple_of(start, LANES), LANES)
+        z = jnp.dot(full[here, :], w_ref[...], preferred_element_type=f32) + bias_ref[...]
+        step = jnp.maximum(z, 0.0) + jnp.log1p(jnp.exp(-jnp.abs(z)))
+        dtb[...] = step
+        vb[...] = step * x_ref[here, :]
+        maps = bc[: 2 * nstate, here].astype(f32) + bc[2 * nstate :, here].astype(f32)
+        for k in range(LANES):
+            bb[k * nstate : (k + 1) * nstate, :] = jnp.broadcast_to(
+                maps[:nstate, k : k + 1], (nstate, LANES)
+            )
+        c = maps[nstate:]
+        c_hi = c.astype(bf16)
+        c_lo = (c - c_hi.astype(f32)).astype(bf16)
+        for i, part in enumerate((c_hi, c_lo)):
+            placed = lax.dot_general(
+                part, spread_map, (((0,), (0,)), ((), ())), preferred_element_type=f32
+            )
+            cx[i] = jnp.where(own, placed, 0.0)
+        rates = [a_ref[g * ROWS : (g + 1) * ROWS, :] for g in range(groups)]
+
+        def tokens(i, states):
+            states = list(states)
+            base = pl.multiple_of(i * ROWS, ROWS)
+            for k in range(ROWS):
+                d = jnp.broadcast_to(dtb[pl.ds(base + k, 1), :], (ROWS, width))
+                v = jnp.broadcast_to(vb[pl.ds(base + k, 1), :], (ROWS, width))
+                row = pl.multiple_of((base + k) * nstate, nstate)
+                for g in range(groups):
+                    b = jnp.tile(bb[pl.ds(row + g * ROWS, ROWS), :], (1, width // LANES))
+                    states[g] = jnp.exp2(d * rates[g]) * states[g] + v * b
+                hb[pl.ds(row, nstate), :] = jnp.concatenate(states, 0).astype(bf16)
+            return tuple(states)
+
+        states = tuple(h_ref[g * ROWS : (g + 1) * ROWS, :] for g in range(groups))
+        states = lax.fori_loop(0, LANES // ROWS, tokens, states)
+        for g in range(groups):
+            h_ref[g * ROWS : (g + 1) * ROWS, :] = states[g]
+        for i in range(LANES // (2 * ROWS)):
+            at = slice(i * 2 * ROWS, (i + 1) * 2 * ROWS)
+            left = jnp.concatenate([cx[0, at, :], cx[1, at, :]], 0).astype(bf16)
+            y = jnp.dot(left, hb[i * wide : (i + 1) * wide, :], preferred_element_type=f32)
+            yb[at, :] = y[: 2 * ROWS] + y[2 * ROWS :]
+        o_ref[here, :] = (
+            p_ref[here, :].astype(f32) + (yb[...] + skip_ref[...] * x_ref[here, :])
+        ).astype(bf16)
+
+    h_ref[...] = jnp.zeros_like(h_ref)
+    greet(axis)
+    for j in range(AHEAD + 1):
+        send_parts(j)
+    for j in range(AHEAD):
+        reduce_and_send(j)
+
+    def block(j, carry):
+        @pl.when(j + AHEAD + 1 < blocks)
+        def _():
+            send_parts(j + AHEAD + 1)
+
+        @pl.when(j + AHEAD < blocks)
+        def _():
+            reduce_and_send(j + AHEAD)
+
+        for k in range(1, n):
+            sum_low(j, k).wait_recv()
+
+        @pl.when(me != j)
+        def _():
+            sum_maps(j, 1).wait_recv()
+
+        for i in range(span // LANES):
+            chunk(j * span + i * LANES)
+        return carry
+
+    lax.fori_loop(0, blocks, block, 0)
+
+    def finish(j, carry):
+        @pl.when(me != j)
+        def _():
+            part_maps(j, me).wait_send()
+
+        for k in range(1, n):
+            part_low(j, k).wait_send()
+            sum_low(j, k).wait_send()
+        return carry
+
+    lax.fori_loop(0, blocks, finish, 0)
+
+    @pl.when(me < blocks)
     def _():
-        h_ref[...] = jnp.zeros_like(h_ref)
-
-    groups = nstate // ROWS
-    chunk = dt_ref.shape[0]
-    tile = (ROWS, dt_ref.shape[1])
-    rates = [a_ref[g * ROWS : (g + 1) * ROWS, :] for g in range(groups)]
-
-    def block(i, states):
-        states = list(states)
-        base = pl.multiple_of(i * ROWS, ROWS)
-        bc = pltpu.roll(bc_ref[...], lax.rem(chunk - i * ROWS, chunk), 1)
-        parts = []
-        for k in range(ROWS):
-            d = jnp.broadcast_to(dt_ref[pl.ds(base + k, 1), :], tile)
-            v = d * jnp.broadcast_to(x_ref[pl.ds(base + k, 1), :], tile)
-            total = None
-            for g in range(groups):
-                b = bc[g * ROWS : (g + 1) * ROWS, k : k + 1]
-                c = bc[nstate + g * ROWS : nstate + (g + 1) * ROWS, k : k + 1]
-                states[g] = jnp.exp2(d * rates[g]) * states[g] + v * b
-                term = states[g] * c
-                total = term if total is None else total + term
-            parts.append(total)
-        o_ref[pl.ds(base, ROWS), :] = folded(parts)
-        return tuple(states)
-
-    states = tuple(h_ref[g * ROWS : (g + 1) * ROWS, :] for g in range(groups))
-    states = lax.fori_loop(0, chunk // ROWS, block, states)
-    for g in range(groups):
-        h_ref[g * ROWS : (g + 1) * ROWS, :] = states[g]
-
-
-def selective_scan(dt, x, bc, rates):
-    length, width = dt.shape
-    nstate = rates.shape[0]
-    chunk = LANES
+        for k in range(1, n):
+            sum_maps(me, k).wait_send()
+
+
+def mix(low, maps, x, present, w, bias, rates, skip, axis, cid):
+    n = lax.axis_size(axis)
+    length, width = x.shape
+    nstate, rank = rates.shape[0], w.shape[0]
+    span = PIECE * n
+    blocks = length // span
+    wide = 2 * ROWS * nstate
+    f32, bf16 = jnp.float32, jnp.bfloat16
+    dma = pltpu.SemaphoreType.DMA
     return pl.pallas_call(
-        functools.partial(scan_kernel, nstate),
-        out_shape=jax.ShapeDtypeStruct((length, width), jnp.float32),
-        grid=(length // chunk,),
-        in_specs=[
-            pl.BlockSpec((chunk, width), lambda i: (i, 0)),
-            pl.BlockSpec((chunk, width), lambda i: (i, 0)),
-            pl.BlockSpec((2 * nstate, chunk), lambda i: (0, i)),
-            pl.BlockSpec((nstate, width), lambda i: (0, 0)),
+        functools.partial(mixer_kernel, axis, nstate),
+        out_shape=jax.ShapeDtypeStruct((length, width), bf16),
+        in_specs=[pl.BlockSpec(memory_space=pltpu.VMEM)] * 8,
+        out_specs=pl.BlockSpec(memory_space=pltpu.VMEM),
+        scratch_shapes=[
+            pltpu.VMEM((length, rank), bf16),
+            pltpu.VMEM((4 * nstate, length), bf16),
+            pltpu.VMEM((blocks, n, PIECE, rank), bf16),
+            pltpu.VMEM((n, 2 * nstate, span), bf16),
+            pltpu.VMEM((LANES, width), f32),
+            pltpu.VMEM((LANES, width), f32),
+            pltpu.VMEM((LANES * nstate, LANES), f32),
+            pltpu.VMEM((2, LANES, wide), f32),
+            pltpu.VMEM((LANES * nstate, width), bf16),
+            pltpu.VMEM((LANES, width), f32),
+            pltpu.VMEM((nstate, width), f32),
+            dma((blocks, n)),
+            dma((blocks, n)),
+            dma((blocks,)),
+            dma((n,)),
+            dma((blocks, n)),
+            dma((blocks, n)),
+            dma((n,)),
+            dma((blocks,)),
         ],
-        out_specs=pl.BlockSpec((chunk, width), lambda i: (i, 0)),
-        scratch_shapes=[pltpu.VMEM((nstate, width), jnp.float32)],
-        compiler_params=pltpu.CompilerParams(vmem_limit_bytes=SMALL_VMEM),
+        compiler_params=pltpu.CompilerParams(
+            collective_id=cid, has_side_effects=True, vmem_limit_bytes=MIX_VMEM
+        ),
         cost_estimate=pl.CostEstimate(
             flops=6 * length * width * nstate,
             bytes_accessed=12 * length * width,
             transcendentals=length * width * nstate,
         ),
-        name="selective_scan",
-    )(dt, x, bc, rates)
+        name=f"mix_{cid}",
+    )(low, maps, x, present, w, bias, rates, skip)
 
 
 def passed_along(x, axis):
@@ -369,7 +485,6 @@
     dt_bias = own(step_size_bias[0], 0)
     rates = -LOG2E * jnp.exp(own(log_decay_rates[0], 0)).T
     skip = own(mixer_skip_weight[0], 0)
-    columns = rank + 2 * nstate
 
     tokens = input_in_transit[0]
     as_float = tokens.astype(f32)
@@ -403,25 +518,28 @@
         for tap in range(kernel):
             convolved = convolved + taps[tap] * padded[tap : tap + length].astype(f32)
         inner = jax.nn.silu(convolved)
-        partial = lax.dot_general(
-            input_projection[0],
-            inner.astype(bf16),
+        inner_b = inner.astype(bf16)
+        low = jnp.dot(
+            inner_b, input_projection[0, :, :rank], preferred_element_type=f32
+        ).astype(bf16)
+        maps = lax.dot_general(
+            input_projection[0, :, rank:],
+            inner_b,
             (((0,), (1,)), ((), ())),
             preferred_element_type=f32,
         ).astype(bf16)
-        everyone = project(partial, rank, rows, "seq", 4)
-        bc = everyone[rank:columns].astype(f32) + everyone[columns:].astype(f32)
-        step_size = jax.nn.softplus(
-            lax.dot_general(
-                everyone[:rank],
-                step_size_projection[0],
-                (((0,), (0,)), ((), ())),
-                preferred_element_type=f32,
-            )
-            + dt_bias
-        )
-        scanned = selective_scan(step_size, inner, bc, rates)
-        mixed = (present.astype(f32) + (scanned + skip * inner)).astype(bf16)
+        mixed = mix(
+            low,
+            maps,
+            inner,
+            present,
+            step_size_projection[0],
+            dt_bias[None],
+            rates,
+            skip[None],
+            "seq",
+            4,
+        )
         dispatch, routed = dispatch_of(all_ids[step], n, capacity)
         picked = jnp.dot(dispatch, mixed, preferred_element_type=f32).astype(bf16)
         last = step + 1 == STEPS

time: 212 us -> 184 us (0.87)
  Pallas kernels: 143 us -> 121 us
  other arithmetic: 11.6 us -> 7.6 us
    pallas_call x4 -> x2, Pallas kernels: 87.1 us -> 63.7 us  [mix(): pl.pallas_call(functools.partial(mixer_kernel, axis, nstate), out_shape=j...]
    convert_element_type x2 -> x0, other arithmetic: 4.34 us -> none  [body(): mixed = (present.astype(f32) + (scanned + skip * inner)).astype(bf16)]
  transfers between devices with their start and end apart: 4 -> 4, of which waited for: 1 -> 1; matrix products, arithmetic and copies ran while one was open for 14% -> 17% of each run, Pallas kernels for 13% -> 15%
where the time goes in v1:
time: 184 us
  Pallas kernels  121 us (66%)
  matrix products  38.7 us (21%)
  starting transfers between devices  7.85 us (4%)
  other arithmetic  7.6 us (4%)
  local copies, waits for them, and re-layouts  4.51 us (2%)
  waiting for transfers between devices  4.17 us (2%)
    pallas_call x2, Pallas kernels, mix(): pl.pallas_call(functools.partial(mixer_kernel, axis, nstate), out_shape=j...  63.7 us
    dot_general x2, matrix products, body(): jnp.dot(hidden, down_weight[0], preferred_element_type=f32).astype(bf16)  25.4 us
    pallas_call x2, Pallas kernels, exchange(): pl.pallas_call(functools.partial(exchange_kernel, axis, parts), out_shape...  21.6 us
    pallas_call x2, Pallas kernels, scatter_sum(): pl.pallas_call(functools.partial(scatter_sum_kernel, axis, src_at), out_s...  18.8 us
    pallas_call x2, Pallas kernels, gather(): pl.pallas_call(functools.partial(gather_kernel, axis, place), out_shape=j...  16.8 us
    dot_general x2, matrix products, body(): gate_part = jnp.dot(moe_in, gate_weight[0], preferred_element_type=f32)  4.71 us
    ppermute x3, starting transfers between devices, passed_along(): return lax.ppermute(x, axis, [(i, (i + 1) % length) for i in range(length)])  4.23 us
    ppermute x3, waiting for transfers between devices, passed_along(): return lax.ppermute(x, axis, [(i, (i + 1) % length) for i in range(length)])  4.16 us
  transfers between devices with their start and end apart: 4, of which 1 were waited for; matrix products, arithmetic and copies ran while one was open for 17% of the time, Pallas kernels for 15%

profile of v1, /device:TPU:1, one launch (start us, length us, event | category | flops | bytes accessed | tf_op | source)
XLA Modules:
  0.0 184.0 jit_solution(17758683937615475086)
XLA Ops:
  0.0 0.0 copy-start
  0.0 0.7 convert_element_type.188
  0.7 1.5 multiply_reduce_fusion
  2.3 1.2 copy-done.1
  3.5 16.7 %exchange_1.1 = (f32[8,8,128]{2,1,0:T(8,128)S(1)}, bf16[1024,512]{1,0:T(8,128)(2,1)S(1)}) custom-call(f32[8,128]{1,0:T(8,128)S(1)} %select_maximum_fusion.refs_0_, bf16[128,4096]{1,0:T(8,128)(2,1)S(1)} %bitcast.164), custom_call_target="tpu_custom_call" | custom-call | tf_op jit(solution)/shard_map/exchange_1/pallas_call | solution.py:62
  20.2 0.7 constant_dynamic-slice_fusion.5
  20.9 0.7 constant_dynamic-slice_fusion.7
  21.6 0.3 multiply_convert_fusion
  21.9 0.0 copy-start.3
  21.9 0.9 constant_dynamic-slice_fusion.2
  22.9 1.4 divide_multiply_fusion.1.x_ref
  24.2 0.0 copy-start.2
  24.2 0.0 slice-start
  24.3 0.5 convolution_convert_fusion.3.low_ref
  24.7 0.4 fusion.38.maps_ref
  25.1 1.2 multiply_bitcast_fusion.a_ref
  26.4 0.7 constant_dynamic-slice_fusion.3
  27.1 31.2 %mix_4.2 = bf16[1024,512]{1,0:T(8,128)(2,1)S(1)} custom-call(bf16[1024,256]{1,0:T(8,128)(2,1)S(1)} %convolution_convert_fusion.3.low_ref, bf16[32,1024]{1,0:T(8,128)(2,1)S(1)} %fusion.38.maps_ref, f32[1024,512]{1,0:T(8,128)S(1)} %divide_multiply_fusion.1.x_ref, bf16[1024,512]{1,0:T(8,128)(2,1)S(1)} %get-tuple-element.8.p_ref, ...), custom_call_target="tpu_custom_call" | custom-call | flops 50331648 | bytes 6291456 | tf_op jit(solution)/shard_map/mix_4/pallas_call | solution.py:393
  58.2 0.0 copy-start.4
  58.3 1.4 collective-permute-start.2
  59.6 1.3 collective-permute-start
  61.0 0.2 fusion.45
  61.2 0.3 convolution_convert_fusion.6.x_ref
  61.5 0.2 fusion.78
  61.7 8.6 %gather_6.2 = bf16[64,4096]{1,0:T(8,128)(2,1)S(1)} custom-call(bf16[64,512]{1,0:T(8,128)(2,1)S(1)} %convolution_convert_fusion.6.x_ref), custom_call_target="tpu_custom_call" | custom-call | tf_op jit(solution)/shard_map/gather_6/pallas_call | solution.py:125
  70.3 0.2 fusion.46
  70.6 0.2 fusion.43
  70.8 0.2 fusion.125
  71.0 0.0 slice-done.2
  71.0 2.4 %fusion.10 = f32[64,1536]{1,0:T(8,128)S(1)} fusion(bf16[1,4096,1536]{2,1,0:T(8,128)(2,1)S(1)} %bitcast.169, bf16[64,4096]{1,0:T(8,128)(2,1)S(1)} %gather_6.2, f32[4096]{0:T(1024)S(1)} %bitcast.174, f32[64]{0:T(128)S(1)} %add_rsqrt_fusion.2), kind=kOutput, calls=%fused_computation.10 | convolution fusion | flops 806354944 | bytes 13517056 | tf_op jit(solution)/shard_map/dot_general | solution.py:574
  73.3 12.7 %fusion.14.x_ref = bf16[64,4096]{1,0:T(8,128)(2,1)S(1)} fusion(bf16[1,1536,4096]{2,1,0:T(8,128)(2,1)} %param.28, bf16[1,4096,1536]{2,1,0:T(8,128)(2,1)} %param.27, f32[64,1536]{1,0:T(8,128)S(1)} %fusion.10, bf16[64,4096]{1,0:T(8,128)(2,1)S(1)} %gather_6.2, f32[4096]{0:T(1024)S(1)} %bitcast.175, f32[64]{0:T(128)S(1)} %add_rsqrt_fusion.2), kind=kOutput, calls=%fused_computation.15 | convolution fusion | flops 1612513280 | bytes 26624256 | tf_op jit(solution)/shard_map/dot_general | solution.py:577
  86.1 9.1 %scatter_sum_7.1 = f32[64,512]{1,0:T(8,128)S(1)} custom-call(bf16[64,4096]{1,0:T(8,128)(2,1)S(1)} %fusion.14.x_ref), custom_call_target="tpu_custom_call" | custom-call | tf_op jit(solution)/shard_map/scatter_sum_7/pallas_call | solution.py:178
  95.2 0.1 compare_convert_fusion
  95.3 0.3 fusion.119
  95.6 0.1 add_convert_fusion.1
  95.7 1.5 collective-permute-start.1
  97.3 0.0 collective-permute-done
  97.4 0.2 fusion.44
  97.6 4.2 %collective-permute-done.1 = bf16[64,512]{1,0:T(8,128)(2,1)S(1)} collective-permute-done((bf16[64,512]{1,0:T(8,128)(2,1)S(1)}, bf16[64,512]{1,0:T(8,128)(2,1)S(1)}, u32[]{:S(2)}, u32[]{:S(2)}) %collective-permute-start.1) | collective-permute-done | bytes 65568 | tf_op jit(solution)/shard_map/ppermute | solution.py:433
  101.7 0.0 collective-permute-done.2
  101.7 1.9 %fusion.35 = (f32[1024]{0:T(1024)S(1)}, bf16[1024,512]{1,0:T(8,128)(2,1)S(1)}) fusion(bf16[1024,512]{1,0:T(8,128)(2,1)} %collective-permute-done.2, bf16[64,512]{1,0:T(8,128)(2,1)S(1)} %collective-permute-done.1, s32[1024]{0:T(1024)S(1)} %fusion.44, pred[1024]{0:T(1024)(128)(4,1)S(1)} %or_reduce_fusion.1), kind=kOutput, calls=%fused_computation.24 | convolution fusion | flops 69860352 | bytes 2171904 | tf_op jit(solution)/shard_map/dot_general | solution.py:595
  103.6 4.9 %exchange_3.1 = f32[8,8,128]{2,1,0:T(8,128)S(1)} custom-call(f32[8,128]{1,0:T(8,128)S(1)} %bitcast.165), custom_call_target="tpu_custom_call" | custom-call | tf_op jit(solution)/shard_map/exchange_3/pallas_call | solution.py:62
  108.5 0.3 fusion.37
  108.8 1.4 divide_multiply_fusion.x_ref
  110.2 0.0 slice-start.3
  110.2 0.5 convolution_convert_fusion.2.low_ref
  110.7 0.4 fusion.39.maps_ref
  111.1 0.0 slice-start.4
  111.1 0.0 slice-start.5
  111.2 32.5 %mix_4.3 = bf16[1024,512]{1,0:T(8,128)(2,1)} custom-call(bf16[1024,256]{1,0:T(8,128)(2,1)S(1)} %convolution_convert_fusion.2.low_ref, bf16[32,1024]{1,0:T(8,128)(2,1)S(1)} %fusion.39.maps_ref, f32[1024,512]{1,0:T(8,128)S(1)} %divide_multiply_fusion.x_ref, bf16[1024,512]{1,0:T(8,128)(2,1)S(1)} %get-tuple-element.24.p_ref, bf16[256,512]{1,0:T(8,128)(2,1)S(1)} %bitcast.167, ...), custom_call_target="tpu_custom_call" | custom-call | flops 50331648 | bytes 6291456 | tf_op jit(solution)/shard_map/mix_4/pallas_call | solution.py:393
  143.7 1.5 convolution_convert_fusion.4.x_ref
  145.2 8.2 %gather_6.3 = bf16[64,4096]{1,0:T(8,128)(2,1)S(1)} custom-call(bf16[64,512]{1,0:T(8,128)(2,1)S(1)} %convolution_convert_fusion.4.x_ref), custom_call_target="tpu_custom_call" | custom-call | tf_op jit(solution)/shard_map/gather_6/pallas_call | solution.py:125
  153.3 0.2 fusion.49
  153.6 0.0 slice-done.4
  153.6 0.0 slice-done.5
  153.6 2.4 %fusion.8 = f32[64,1536]{1,0:T(8,128)S(1)} fusion(bf16[1,4096,1536]{2,1,0:T(8,128)(2,1)S(1)} %bitcast.171, bf16[64,4096]{1,0:T(8,128)(2,1)S(1)} %gather_6.3, f32[64]{0:T(128)S(1)} %add_rsqrt_fusion.1, f32[4096]{0:T(1024)S(1)} %bitcast.177), kind=kOutput, calls=%fused_computation.8 | convolution fusion | flops 806354944 | bytes 13517056 | tf_op jit(solution)/shard_map/dot_general | solution.py:574
  156.0 3.6 %all-to-all-start = ((bf16[8,128,512]{2,1,0:T(8,128)(2,1)}), bf16[8,128,512]{2,1,0:T(8,128)(2,1)S(1)}, u32[]{:S(2)}, u32[]{:S(2)}) async-start(bf16[8,128,512]{2,1,0:T(8,128)(2,1)} %bitcast.44), calls=%async_computation | async-start | bytes 2097152 | tf_op jit(solution)/shard_map/all_to_all | solution.py:551
  159.6 12.7 %fusion.20.x_ref = bf16[8,8,4096]{2,1,0:T(8,128)(2,1)S(1)} fusion(bf16[1,1536,4096]{2,1,0:T(8,128)(2,1)} %param.28, bf16[1,4096,1536]{2,1,0:T(8,128)(2,1)} %param.27, f32[64,1536]{1,0:T(8,128)S(1)} %fusion.8, bf16[64,4096]{1,0:T(8,128)(2,1)S(1)} %gather_6.3, f32[64]{0:T(128)S(1)} %add_rsqrt_fusion.1, f32[4096]{0:T(1024)S(1)} %bitcast.178), kind=kOutput, calls=%fused_computation.17 | convolution fusion | flops 1612513280 | bytes 26624256 | tf_op jit(solution)/shard_map/dot_general | solution.py:577
  172.3 9.7 %scatter_sum_8.1 = f32[8,4096]{1,0:T(8,128)S(1)} custom-call(bf16[8,8,4096]{2,1,0:T(8,128)(2,1)S(1)} %fusion.20.x_ref), custom_call_target="tpu_custom_call" | custom-call | tf_op jit(solution)/shard_map/scatter_sum_8/pallas_call | solution.py:178
  182.0 0.3 fusion.115
  182.3 0.1 dynamic_slice.42
  182.4 0.0 all-to-all-done
  182.4 0.1 copy.17
  182.5 1.5 fusion.13
  (29 shorter events, 0.3 us)
Async XLA Ops:
  0.0 95.3 %copy-start = (bf16[1,4096,16]{1,2,0:T(8,128)(2,1)S(1)}, bf16[1,4096,16]{1,2,0:T(8,128)(2,1)}, u32[]{:S(2)}) copy-start(bf16[1,4096,16]{1,2,0:T(8,128)(2,1)} %param.25) | copy-start | bytes 393220
  2.3 1.2 copy-start.1
  21.9 2.3 %copy-start.3 = (bf16[1,512,288]{1,2,0:T(8,128)(2,1)S(1)}, bf16[1,512,288]{1,2,0:T(8,128)(2,1)}, u32[]{:S(2)}) copy-start(bf16[1,512,288]{1,2,0:T(8,128)(2,1)} %param.19) | copy-start | bytes 884740
  24.2 2.8 %copy-start.2 = (bf16[1,256,512]{2,1,0:T(8,128)(2,1)S(1)}, bf16[1,256,512]{2,1,0:T(8,128)(2,1)}, u32[]{:S(2)}) copy-start(bf16[1,256,512]{2,1,0:T(8,128)(2,1)} %param.20) | copy-start | bytes 786436
  24.2 46.7 %slice-start = ((s8[12582912]{0:T(1024)(128)(4,1)}), s8[4194304]{0:T(1024)(128)(4,1)S(1)}, s32[]{:S(2)}) async-start(s8[12582912]{0:T(1024)(128)(4,1)} %bitcast.168), calls=%async_computation.1 | async-start | bytes 8388608
  27.1 43.9 %slice-start.1 = ((s8[12582912]{0:T(1024)(128)(4,1)}), s8[4194304]{0:T(1024)(128)(4,1)S(1)}, s32[]{:S(2)}) async-start(s8[12582912]{0:T(1024)(128)(4,1)} %bitcast.168), calls=%async_computation.2 | async-start | bytes 8388608
  27.1 43.9 %slice-start.2 = ((s8[12582912]{0:T(1024)(128)(4,1)}), s8[4194304]{0:T(1024)(128)(4,1)S(1)}, s32[]{:S(2)}) async-start(s8[12582912]{0:T(1024)(128)(4,1)} %bitcast.168), calls=%async_computation.3 | async-start | bytes 8388608
  58.2 12.7 %copy-start.4 = (f32[1,4096]{1,0:T(1,128)S(1)}, f32[1,4096]{1,0:T(1,128)}, u32[]{:S(2)}) copy-start(f32[1,4096]{1,0:T(1,128)} %param.24) | copy-start | bytes 49156
  58.3 43.5 %collective-permute-start.2 = (bf16[1024,512]{1,0:T(8,128)(2,1)S(1)}, bf16[1024,512]{1,0:T(8,128)(2,1)}, u32[]{:S(2)}, u32[]{:S(2)}) collective-permute-start(bf16[1024,512]{1,0:T(8,128)(2,1)S(1)} %mix_4.2), channel_id=1, source_target_pairs={{0,8},{8,16},{16,24},{24,0},{1,9},{9,17},{17,25},{25,1},{2,10},{10... | collective-permute-start | bytes 3145736 | tf_op jit(solution)/shard_map/ppermute | solution.py:433
  59.6 37.7 %collective-permute-start = (f32[1024,2]{0,1:T(2,128)S(1)}, f32[1024,2]{0,1:T(2,128)S(1)}, u32[]{:S(2)}, u32[]{:S(2)}) collective-permute-start(f32[1024,2]{0,1:T(2,128)S(1)} %get-tuple-element.20), channel_id=1, source_target_pairs={{0,8},{8,16},{16,24},{24,0},{1,9},{9,17},{17,25},{25,1},{2,10},{10... | collective-permute-start | bytes 24584 | tf_op jit(solution)/shard_map/ppermute | solution.py:433
  95.7 6.0 %collective-permute-start.1 = (bf16[64,512]{1,0:T(8,128)(2,1)S(1)}, bf16[64,512]{1,0:T(8,128)(2,1)S(1)}, u32[]{:S(2)}, u32[]{:S(2)}) collective-permute-start(bf16[64,512]{1,0:T(8,128)(2,1)S(1)} %add_convert_fusion.1), channel_id=1, source_target_pairs={{0,8},{8,16},{16,24},{24,0},{1,9},{9,17},{17,25},{25,1},{2,10},{10... | collective-permute-start | bytes 196616 | tf_op jit(solution)/shard_map/ppermute | solution.py:433
  110.2 43.3 %slice-start.3 = ((s8[12582912]{0:T(1024)(128)(4,1)}), s8[4194304]{0:T(1024)(128)(4,1)S(1)}, s32[]{:S(2)}) async-start(s8[12582912]{0:T(1024)(128)(4,1)} %bitcast.170), calls=%async_computation.4 | async-start | bytes 8388608
  111.1 42.4 %slice-start.4 = ((s8[12582912]{0:T(1024)(128)(4,1)}), s8[4194304]{0:T(1024)(128)(4,1)S(1)}, s32[]{:S(2)}) async-start(s8[12582912]{0:T(1024)(128)(4,1)} %bitcast.170), calls=%async_computation.5 | async-start | bytes 8388608
  111.1 42.4 %slice-start.5 = ((s8[12582912]{0:T(1024)(128)(4,1)}), s8[4194304]{0:T(1024)(128)(4,1)S(1)}, s32[]{:S(2)}) async-start(s8[12582912]{0:T(1024)(128)(4,1)} %bitcast.170), calls=%async_computation.6 | async-start | bytes 8388608
  156.0 26.5 %all-to-all-start = ((bf16[8,128,512]{2,1,0:T(8,128)(2,1)}), bf16[8,128,512]{2,1,0:T(8,128)(2,1)S(1)}, u32[]{:S(2)}, u32[]{:S(2)}) async-start(bf16[8,128,512]{2,1,0:T(8,128)(2,1)} %bitcast.44), calls=%async_computation | async-start | bytes 2097152 | tf_op jit(solution)/shard_map/all_to_all | solution.py:551

commit v2 on v1

--- a/solution.py
+++ b/solution.py
@@ -16,6 +16,7 @@
 MIX_VMEM = 24 * 1024 * 1024
 PIECE = 16
 AHEAD = 2
+EXPERT_VMEM = 46 * 1024 * 1024
 
 
 def greet(axis):
@@ -114,78 +115,6 @@
 
 def spread_scratch(n):
     return [pltpu.SemaphoreType.DMA((n // 2,))] * 4 + [pltpu.SemaphoreType.DMA]
-
-
-def gather_kernel(axis, place, x_ref, o_ref, *sems):
-    greet(axis)
-    spread(axis, x_ref, place, o_ref, *sems)
-
-
-def gather(x, shape, place, axis, cid):
-    return pl.pallas_call(
-        functools.partial(gather_kernel, axis, place),
-        out_shape=jax.ShapeDtypeStruct(shape, x.dtype),
-        in_specs=[pl.BlockSpec(memory_space=pl.ANY)],
-        out_specs=pl.BlockSpec(memory_space=pl.ANY),
-        scratch_shapes=spread_scratch(lax.axis_size(axis)),
-        compiler_params=pltpu.CompilerParams(
-            collective_id=cid, has_side_effects=True, vmem_limit_bytes=SMALL_VMEM
-        ),
-        name=f"gather_{cid}",
-    )(x)
-
-
-def reduce_here(axis, src_at, x_ref, held, send_sem, recv_sem, local_sem):
-    n, me = lax.axis_size(axis), lax.axis_index(axis)
-    copies = []
-    for k in range(1, n):
-        peer = lax.rem(me + k, n)
-        copy = pltpu.make_async_remote_copy(
-            src_ref=src_at(x_ref, peer),
-            dst_ref=held.at[k],
-            send_sem=send_sem.at[k],
-            recv_sem=recv_sem.at[k],
-            device_id={axis: peer},
-            device_id_type=MESH,
-        )
-        copy.start()
-        copies.append(copy)
-    own = pltpu.make_async_copy(src_at(x_ref, me), held.at[0], local_sem)
-    own.start()
-    own.wait()
-    total = held[0].astype(jnp.float32)
-    for k in range(1, n):
-        copies[k - 1].wait()
-        total = total + held[k].astype(jnp.float32)
-    return total
-
-
-def reduce_scratch(n, shape, dtype):
-    return [
-        pltpu.VMEM((n,) + shape, dtype),
-        pltpu.SemaphoreType.DMA((n,)),
-        pltpu.SemaphoreType.DMA((n,)),
-        pltpu.SemaphoreType.DMA,
-    ]
-
-
-def scatter_sum_kernel(axis, src_at, x_ref, o_ref, *scratch):
-    greet(axis)
-    o_ref[...] = reduce_here(axis, src_at, x_ref, *scratch)
-
-
-def scatter_sum(x, shape, src_at, axis, cid):
-    return pl.pallas_call(
-        functools.partial(scatter_sum_kernel, axis, src_at),
-        out_shape=jax.ShapeDtypeStruct(shape, jnp.float32),
-        in_specs=[pl.BlockSpec(memory_space=pl.ANY)],
-        out_specs=pl.BlockSpec(memory_space=pltpu.VMEM),
-        scratch_shapes=reduce_scratch(lax.axis_size(axis), shape, x.dtype),
-        compiler_params=pltpu.CompilerParams(
-            collective_id=cid, has_side_effects=True, vmem_limit_bytes=SMALL_VMEM
-        ),
-        name=f"scatter_sum_{cid}",
-    )(x)
 
 
 def row_block(size):
@@ -426,6 +355,178 @@
         ),
         name=f"mix_{cid}",
     )(low, maps, x, present, w, bias, rates, skip)
+
+
+def expert_kernel(
+    axis, last, columns, picked_ref, gain_ref, router_ref, choice_ref, marks_ref, gate_hbm, up_hbm, down_hbm,
+    *refs,
+):
+    n, me = lax.axis_size(axis), lax.axis_index(axis)
+    f32, bf16 = jnp.float32, jnp.bfloat16
+    slots, width = picked_ref.shape
+    model, ff = gate_hbm.shape
+    pieces = ff // columns
+    if last:
+        o_ref, route_ref, full = refs[:3]
+        refs = refs[3:]
+    else:
+        o_ref, full = refs[:2]
+        refs = refs[2:]
+    moe_in, hidden, gate, up, down, terms, held = refs[:7]
+    gate_sem, up_sem, down_sem, out_sem, in_sem = refs[7:12]
+    sems = refs[12:]
+
+    def fetch_in(hbm, buf, sem, i):
+        at = pl.ds(pl.multiple_of(i * columns, columns), columns)
+        return pltpu.make_async_copy(hbm.at[:, at], buf.at[i], sem.at[i])
+
+    def fetch_down(k):
+        block = k if last else lax.rem(me + k, n)
+        at = pl.ds(pl.multiple_of(block * width, width), width)
+        return pltpu.make_async_copy(down_hbm.at[:, at], down.at[k], down_sem.at[k])
+
+    for i in range(pieces):
+        fetch_in(gate_hbm, gate, gate_sem, i).start()
+        fetch_in(up_hbm, up, up_sem, i).start()
+    for k in range(n):
+        fetch_down(k if last else (k + 1) % n).start()
+
+    greet(axis)
+    spread(axis, picked_ref, column_block(width), full, *sems)
+
+    square = jnp.zeros((slots, 1), f32)
+    for i in range(0, model, columns):
+        part = full[:, i : i + columns].astype(f32)
+        square = square + jnp.sum(part * part, axis=1, keepdims=True)
+    scale = lax.rsqrt(square / model + 1e-06)
+    for i in range(0, model, columns):
+        at = slice(i, i + columns)
+        moe_in[:, at] = (full[:, at].astype(f32) * scale * gain_ref[:, at]).astype(bf16)
+
+    def piece(i, carry):
+        fetch_in(gate_hbm, gate, gate_sem, i).wait()
+        gate_part = jnp.dot(moe_in[...], gate[i], preferred_element_type=f32)
+        fetch_in(up_hbm, up, up_sem, i).wait()
+        up_part = jnp.dot(moe_in[...], up[i], preferred_element_type=f32)
+        at = pl.ds(pl.multiple_of(i * columns, columns), columns)
+        hidden[:, at] = (gate_part * jax.nn.sigmoid(gate_part) * up_part).astype(bf16)
+        return carry
+
+    lax.fori_loop(0, pieces, piece, 0)
+
+    def term(k):
+        fetch_down(k).wait()
+        return jnp.dot(hidden[...], down[k], preferred_element_type=f32)
+
+    def to(peer, source, target, i, k):
+        return pltpu.make_async_remote_copy(
+            src_ref=source,
+            dst_ref=target,
+            send_sem=out_sem.at[i, k],
+            recv_sem=in_sem.at[i, k],
+            device_id={axis: peer},
+            device_id_type=MESH,
+        )
+
+    half = model // 2
+
+    def part_of(k, i):
+        peer = lax.rem(me + k, n)
+        if not last:
+            return to(peer, terms.at[k], held.at[k], 0, k)
+        at = pl.ds(i * half, half)
+        return to(peer, terms.at[peer, :, at], held.at[k, :, at], i, k)
+
+    def route():
+        logits = lax.dot_general(
+            moe_in[...], router_ref[...], (((1,), (1,)), ((), ())), preferred_element_type=f32
+        )
+        one = jax.nn.sigmoid(jnp.sum(logits * choice_ref[...], axis=1, keepdims=True))
+        marks = marks_ref[...]
+        return marks[:, 0:1] * one + marks[:, 1:2] * (1.0 - one)
+
+    if last:
+        capacity = slots // n
+
+        def rows(q, carry):
+            at = pl.ds(pl.multiple_of(q * width, width), width)
+            terms[:, :, at] = term(q).reshape(n, capacity, width).astype(bf16)
+            return carry
+
+        for i in range(2):
+            lax.fori_loop(i * n // 2, (i + 1) * n // 2, rows, 0)
+            for k in range(1, n):
+                part_of(k, i).start()
+        route_ref[...] = route()
+        total = terms[me].astype(f32)
+        for k in range(1, n):
+            for i in range(2):
+                part_of(k, i).wait()
+            total = total + held[k].astype(f32)
+        o_ref[...] = total.astype(bf16)
+    else:
+
+        def block(k, carry):
+            terms[k] = term(k).astype(bf16)
+            part_of(k, 0).start()
+            return carry
+
+        lax.fori_loop(1, n, block, 0)
+        total = term(0).astype(bf16).astype(f32)
+        weight = route()
+        for k in range(1, n):
+            part_of(k, 0).wait()
+            total = total + held[k].astype(f32)
+        expert_out = total.astype(bf16).astype(f32)
+        o_ref[...] = (picked_ref[...].astype(f32) + weight * expert_out).astype(bf16)
+
+
+def expert(picked, gain, router, choice, marks, gate, up, down, last, axis, cid):
+    n = lax.axis_size(axis)
+    slots, width = picked.shape
+    model, ff = gate.shape
+    columns = 512 if ff % 512 == 0 else ff
+    f32, bf16 = jnp.float32, jnp.bfloat16
+    dma = pltpu.SemaphoreType.DMA
+    vmem = pl.BlockSpec(memory_space=pltpu.VMEM)
+    hbm = pl.BlockSpec(memory_space=pltpu.HBM)
+    part = (slots // n, model) if last else (slots, width)
+    rows = jax.ShapeDtypeStruct(part, bf16)
+    full = jax.ShapeDtypeStruct((slots, model), bf16)
+    if last:
+        out_shape = [rows, jax.ShapeDtypeStruct((slots, 1), f32), full]
+    else:
+        out_shape = [rows, full]
+    return pl.pallas_call(
+        functools.partial(expert_kernel, axis, last, columns),
+        out_shape=out_shape,
+        in_specs=[vmem] * 5 + [hbm] * 3,
+        out_specs=[vmem] * len(out_shape),
+        scratch_shapes=[
+            pltpu.VMEM((slots, model), bf16),
+            pltpu.VMEM((slots, ff), bf16),
+            pltpu.VMEM((ff // columns, model, columns), bf16),
+            pltpu.VMEM((ff // columns, model, columns), bf16),
+            pltpu.VMEM((n, ff, width), bf16),
+            pltpu.VMEM((n,) + part, bf16),
+            pltpu.VMEM((n,) + part, bf16),
+            dma((ff // columns,)),
+            dma((ff // columns,)),
+            dma((n,)),
+            dma((2, n)),
+            dma((2, n)),
+        ]
+        + spread_scratch(n),
+        compiler_params=pltpu.CompilerParams(
+            collective_id=cid, has_side_effects=True, vmem_limit_bytes=EXPERT_VMEM
+        ),
+        cost_estimate=pl.CostEstimate(
+            flops=6 * slots * model * ff,
+            bytes_accessed=6 * model * ff,
+            transcendentals=slots * ff,
+        ),
+        name=f"expert_{cid}",
+    )(picked, gain, router, choice, marks, gate, up, down)
 
 
 def passed_along(x, axis):
@@ -546,50 +647,43 @@
         if not last:
             moved = passed_along(mixed, "section")
             moved_ids = passed_along(all_ids[step], "section")
-        full = gather(picked, (slots, model), column_block(width), "seq", 6)
         if last:
             mixed = lax.all_to_all(
                 mixed.reshape(n, rows, width), "seq", split_axis=0, concat_axis=0
             )
             mixed = mixed.transpose(1, 0, 2).reshape(rows, model)
-        full_float = full.astype(f32)
-        moe_in = (
-            full_float
-            * lax.rsqrt(jnp.mean(full_float * full_float, axis=-1, keepdims=True) + 1e-06)
-            * expert_norm_gain[0]
-        ).astype(bf16)
-        logits = jnp.dot(moe_in, router[0], preferred_element_type=f32)
         slot_ids = jnp.dot(dispatch, all_ids[step].astype(bf16), preferred_element_type=f32)
         one_hot = (
             slot_ids[:, :, None] == jnp.arange(experts, dtype=jnp.int32).astype(f32)
         ).astype(f32)
-        first = jnp.sum(logits * one_hot[:, 0], axis=1)
-        second = jnp.sum(logits * one_hot[:, 1], axis=1)
-        weight_one = jax.nn.sigmoid(first - second)
-        route = jnp.where(
-            slot_ids[:, 0] == 0,
-            weight_one,
-            jnp.where(slot_ids[:, 1] == 0, 1.0 - weight_one, jnp.zeros_like(weight_one)),
-        )
-        gate_part = jnp.dot(moe_in, gate_weight[0], preferred_element_type=f32)
-        up_part = jnp.dot(moe_in, up_weight[0], preferred_element_type=f32)
-        hidden = (jax.nn.silu(gate_part) * up_part).astype(bf16)
-        terms = jnp.dot(hidden, down_weight[0], preferred_element_type=f32).astype(bf16)
+        choice = one_hot[:, 0] - one_hot[:, 1]
+        is_first = slot_ids[:, 0] == 0
+        is_second = (slot_ids[:, 1] == 0) & ~is_first
+        marks = jnp.stack([is_first, is_second], 1).astype(f32)
+        outs = expert(
+            picked,
+            expert_norm_gain,
+            router[0].T,
+            choice,
+            marks,
+            gate_weight[0],
+            up_weight[0],
+            down_weight[0],
+            last,
+            "seq",
+            8 if last else 7,
+        )
         if last:
-            terms = terms.reshape(n, capacity, model)
-            expert_out = scatter_sum(terms, (capacity, model), slot_of, "seq", 8)
+            expert_out, route, full = outs
             dispatch = lax.dynamic_slice(
                 dispatch, (me * capacity, me * rows), (capacity, rows)
             )
             routed = lax.dynamic_slice_in_dim(routed, me * rows, rows, 0)
             route = lax.dynamic_slice_in_dim(route, me * capacity, capacity, 0)
             picked = lax.dynamic_slice_in_dim(full, me * capacity, capacity, 0)
+            new_rows = (picked.astype(f32) + route * expert_out.astype(f32)).astype(bf16)
         else:
-            expert_out = scatter_sum(terms, (slots, width), column_block(width), "seq", 7)
-        expert_out = expert_out.astype(bf16).astype(f32)
-        new_rows = (picked.astype(f32) + route[:, None] * expert_out).astype(bf16)
-        if not last:
-            new_rows = passed_along(new_rows, "section")
+            new_rows = passed_along(outs[0], "section")
             dispatch, routed = dispatch_of(moved_ids, n, capacity)
             mixed = moved
         placed = lax.dot_general(

time: 184 us -> 172 us (0.935)
  matrix products: 38.7 us -> 7.89 us
  Pallas kernels: 121 us -> 141 us
    dot_general x6 -> x0, matrix products: 30.8 us -> none  [the longest x2 25.4 us: body(): jnp.dot(hidden, down_weight[0], preferred_element_type=f32).astype(bf16)]
    pallas_call x4 -> x2, Pallas kernels: 35.6 us -> 55.9 us  [expert(): pl.pallas_call(functools.partial(expert_kernel, axis, last, columns), out...]
  transfers between devices with their start and end apart: 4 -> 4, of which waited for: 1 -> 1; matrix products, arithmetic and copies ran while one was open for 17% -> 2% of each run, Pallas kernels for 15% -> 33%
where the time goes in v2:
time: 172 us; the launch traced here: 171 us
  Pallas kernels  141 us (82%)
  matrix products  7.89 us (5%)
  starting transfers between devices  7.62 us (4%)
  other arithmetic  6.68 us (4%)
  local copies, waits for them, and re-layouts  4.02 us (2%)
  waiting for transfers between devices  4.02 us (2%)
    pallas_call x2, Pallas kernels, mix(): pl.pallas_call(functools.partial(mixer_kernel, axis, nstate), out_shape=j...  63.5 us
    pallas_call x2, Pallas kernels, expert(): pl.pallas_call(functools.partial(expert_kernel, axis, last, columns), out...  55.9 us
    pallas_call x2, Pallas kernels, exchange(): pl.pallas_call(functools.partial(exchange_kernel, axis, parts), out_shape...  21.3 us
    ppermute x3, waiting for transfers between devices, passed_along(): return lax.ppermute(x, axis, [(i, (i + 1) % length) for i in range(length)])  4.01 us
    all_to_all x1, starting transfers between devices, body(): lax.all_to_all(mixed.reshape(n, rows, width), 'seq', split_axis=0, concat...  3.97 us
    ppermute x3, starting transfers between devices, passed_along(): return lax.ppermute(x, axis, [(i, (i + 1) % length) for i in range(length)])  3.65 us
  transfers between devices with their start and end apart: 4, of which 1 were waited for; matrix products, arithmetic and copies ran while one was open for 2% of the time, Pallas kernels for 33%

profile of v2, /device:TPU:1, one launch (start us, length us, event | category | flops | bytes accessed | tf_op | source)
XLA Modules:
  0.0 171.1 jit_solution(15363887001147482924)
XLA Ops:
  0.0 0.0 copy-start
  0.0 0.7 convert_element_type.155
  0.7 1.5 multiply_reduce_fusion
  2.2 0.0 copy-start.1
  2.2 1.2 copy-done.1
  3.5 16.7 %exchange_1.1 = (f32[8,8,128]{2,1,0:T(8,128)S(1)}, bf16[1024,512]{1,0:T(8,128)(2,1)S(1)}) custom-call(f32[8,128]{1,0:T(8,128)S(1)} %select_maximum_fusion.refs_0_, bf16[128,4096]{1,0:T(8,128)(2,1)S(1)} %bitcast.92), custom_call_target="tpu_custom_call" | custom-call | tf_op jit(solution)/shard_map/exchange_1/pallas_call | solution.py:63
  20.2 0.0 copy-done
  20.2 0.7 constant_dynamic-slice_fusion.7
  20.9 0.3 multiply_convert_fusion
  21.2 0.0 copy-start.5
  21.2 0.9 constant_dynamic-slice_fusion.2
  22.2 1.4 divide_multiply_fusion.1.x_ref
  23.5 0.0 copy-done.5
  23.6 0.0 copy-start.4
  23.6 0.5 convolution_convert_fusion.3.low_ref
  24.0 0.4 fusion.5.maps_ref
  24.5 0.8 multiply_bitcast_fusion.a_ref
  25.2 0.7 constant_dynamic-slice_fusion.3
  26.0 0.0 copy-done.4
  26.0 0.0 copy-start.3
  26.0 31.2 %mix_4.2 = bf16[1024,512]{1,0:T(8,128)(2,1)S(1)} custom-call(bf16[1024,256]{1,0:T(8,128)(2,1)S(1)} %convolution_convert_fusion.3.low_ref, bf16[32,1024]{1,0:T(8,128)(2,1)S(1)} %fusion.5.maps_ref, f32[1024,512]{1,0:T(8,128)S(1)} %divide_multiply_fusion.1.x_ref, bf16[1024,512]{1,0:T(8,128)(2,1)S(1)} %get-tuple-element.12.p_ref, bf16[256,512]{1,0:T(8,128)(2,1)S(1)} %bitcast.96, ...), custom_call_target="tpu_custom_call" | custom-call | flops 50331648 | bytes 6291456 | tf_op jit(solution)/shard_map/mix_4/pallas_call | solution.py:322
  57.1 0.0 copy-start.2
  57.2 1.3 collective-permute-start.2
  58.5 1.4 collective-permute-start
  59.9 0.2 fusion.12
  60.2 0.2 fusion.10
  60.4 0.2 fusion.59
  60.6 0.2 fusion.25
  60.7 0.1 compare_convert_fusion
  60.9 0.1 copy.29.marks_ref
  61.0 0.3 convolution_convert_fusion.6.picked_ref
  61.3 0.0 copy-done.3
  61.3 0.0 copy-done.2
  61.3 24.2 %expert_7.1 = (bf16[64,512]{1,0:T(8,128)(2,1)S(1)}, bf16[64,4096]{1,0:T(8,128)(2,1)}) custom-call(bf16[64,512]{1,0:T(8,128)(2,1)S(1)} %convolution_convert_fusion.6.picked_ref, f32[1,4096]{1,0:T(1,128)S(1)} %copy-done.3, bf16[16,4096]{1,0:T(8,128)(2,1)S(1)} %bitcast.93, f32[64,16]{1,0:T(8,128)S(1)} %get-tuple-element.36.choice_ref, ...), custom_call_target="tpu_custom_call" | custom-call | flops 2415919104 | bytes 37748736 | tf_op jit(solution)/shard_map/expert_7/pallas_call | solution.py:500
  85.5 0.9 collective-permute-start.1
  86.5 0.0 collective-permute-done
  86.5 0.2 fusion.11
  86.7 4.0 %collective-permute-done.1 = bf16[64,512]{1,0:T(8,128)(2,1)S(1)} collective-permute-done((bf16[64,512]{1,0:T(8,128)(2,1)S(1)}, bf16[64,512]{1,0:T(8,128)(2,1)S(1)}, u32[]{:S(2)}, u32[]{:S(2)}) %collective-permute-start.1) | collective-permute-done | bytes 65568 | tf_op jit(solution)/shard_map/ppermute | solution.py:534
  90.7 0.0 collective-permute-done.2
  90.7 1.9 %fusion.2 = (f32[1024]{0:T(1024)S(1)}, bf16[1024,512]{1,0:T(8,128)(2,1)S(1)}) fusion(bf16[1024,512]{1,0:T(8,128)(2,1)} %collective-permute-done.2, bf16[64,512]{1,0:T(8,128)(2,1)S(1)} %collective-permute-done.1, s32[1024]{0:T(1024)S(1)} %fusion.11, pred[1024]{0:T(1024)(128)(4,1)S(1)} %or_reduce_fusion.1), kind=kOutput, calls=%fused_computation.5 | convolution fusion | flops 69860352 | bytes 2171904 | tf_op jit(solution)/shard_map/dot_general | solution.py:689
  92.6 4.5 %exchange_3.1 = f32[8,8,128]{2,1,0:T(8,128)S(1)} custom-call(f32[8,128]{1,0:T(8,128)S(1)} %bitcast.95), custom_call_target="tpu_custom_call" | custom-call | tf_op jit(solution)/shard_map/exchange_3/pallas_call | solution.py:63
  97.2 0.3 fusion.4
  97.5 1.4 divide_multiply_fusion.x_ref
  98.9 0.5 convolution_convert_fusion.2.low_ref
  99.4 0.4 fusion.6.maps_ref
  99.8 32.3 %mix_4.3 = bf16[1024,512]{1,0:T(8,128)(2,1)} custom-call(bf16[1024,256]{1,0:T(8,128)(2,1)S(1)} %convolution_convert_fusion.2.low_ref, bf16[32,1024]{1,0:T(8,128)(2,1)S(1)} %fusion.6.maps_ref, f32[1024,512]{1,0:T(8,128)S(1)} %divide_multiply_fusion.x_ref, bf16[1024,512]{1,0:T(8,128)(2,1)S(1)} %get-tuple-element.32.p_ref, bf16[256,512]{1,0:T(8,128)(2,1)S(1)} %bitcast.97, ...), custom_call_target="tpu_custom_call" | custom-call | flops 50331648 | bytes 6291456 | tf_op jit(solution)/shard_map/mix_4/pallas_call | solution.py:322
  132.1 4.0 %all-to-all-start = ((bf16[8,128,512]{2,1,0:T(8,128)(2,1)}), bf16[8,128,512]{2,1,0:T(8,128)(2,1)S(1)}, u32[]{:S(2)}, u32[]{:S(2)}) async-start(bf16[8,128,512]{2,1,0:T(8,128)(2,1)} %bitcast.37), calls=%async_computation | async-start | bytes 2097152 | tf_op jit(solution)/shard_map/all_to_all | solution.py:651
  136.1 0.1 copy.30.marks_ref
  136.2 1.5 convolution_convert_fusion.4.picked_ref
  137.7 31.7 %expert_8.1 = (bf16[8,4096]{1,0:T(8,128)(2,1)S(1)}, f32[64,1]{1,0:T(8,128)S(1)}, bf16[64,4096]{1,0:T(8,128)(2,1)S(1)}) custom-call(bf16[64,512]{1,0:T(8,128)(2,1)S(1)} %convolution_convert_fusion.4.picked_ref, f32[1,4096]{1,0:T(1,128)S(1)} %copy-done.3, bf16[16,4096]{1,0:T(8,128)(2,1)S(1)} %bitcast.94, f32[64,16]{1,0:T(8,128)S(1)} %get-tuple-element.35.choice_ref, ...), custom_call_target="tpu_custom_call" | custom-call | flops 2415919104 | bytes 37748736 | tf_op jit(solution)/shard_map/expert_8/pallas_call | solution.py:500
  169.4 0.1 dynamic-slice_reduce_fusion
  169.5 0.0 all-to-all-done
  169.5 0.1 copy.32
  169.6 1.5 fusion.1
  (19 shorter events, 0.3 us)
Async XLA Ops:
  0.0 20.2 %copy-start = (f32[1,4096]{1,0:T(1,128)S(1)}, f32[1,4096]{1,0:T(1,128)}, u32[]{:S(2)}) copy-start(f32[1,4096]{1,0:T(1,128)} %param.16) | copy-start | bytes 49156
  2.2 1.2 copy-start.1
  21.2 2.3 %copy-start.5 = (bf16[1,512,288]{1,2,0:T(8,128)(2,1)S(1)}, bf16[1,512,288]{1,2,0:T(8,128)(2,1)}, u32[]{:S(2)}) copy-start(bf16[1,512,288]{1,2,0:T(8,128)(2,1)} %param.19) | copy-start | bytes 884740
  23.6 2.4 %copy-start.4 = (bf16[1,256,512]{2,1,0:T(8,128)(2,1)S(1)}, bf16[1,256,512]{2,1,0:T(8,128)(2,1)}, u32[]{:S(2)}) copy-start(bf16[1,256,512]{2,1,0:T(8,128)(2,1)} %param.20) | copy-start | bytes 786436
  26.0 35.3 %copy-start.3 = (f32[1,4096]{1,0:T(1,128)S(1)}, f32[1,4096]{1,0:T(1,128)}, u32[]{:S(2)}) copy-start(f32[1,4096]{1,0:T(1,128)} %gain_ref.3) | copy-start | bytes 49156
  57.1 4.1 %copy-start.2 = (bf16[1,4096,16]{1,2,0:T(8,128)(2,1)S(1)}, bf16[1,4096,16]{1,2,0:T(8,128)(2,1)}, u32[]{:S(2)}) copy-start(bf16[1,4096,16]{1,2,0:T(8,128)(2,1)} %param.25) | copy-start | bytes 393220
  57.2 33.6 %collective-permute-start.2 = (bf16[1024,512]{1,0:T(8,128)(2,1)S(1)}, bf16[1024,512]{1,0:T(8,128)(2,1)}, u32[]{:S(2)}, u32[]{:S(2)}) collective-permute-start(bf16[1024,512]{1,0:T(8,128)(2,1)S(1)} %mix_4.2), channel_id=1, source_target_pairs={{0,8},{8,16},{16,24},{24,0},{1,9},{9,17},{17,25},{25,1},{2,10},{10... | collective-permute-start | bytes 3145736 | tf_op jit(solution)/shard_map/ppermute | solution.py:534
  58.5 28.0 %collective-permute-start = (f32[1024,2]{0,1:T(2,128)S(1)}, f32[1024,2]{0,1:T(2,128)S(1)}, u32[]{:S(2)}, u32[]{:S(2)}) collective-permute-start(f32[1024,2]{0,1:T(2,128)S(1)} %get-tuple-element.24), channel_id=1, source_target_pairs={{0,8},{8,16},{16,24},{24,0},{1,9},{9,17},{17,25},{25,1},{2,10},{10... | collective-permute-start | bytes 24584 | tf_op jit(solution)/shard_map/ppermute | solution.py:534
  85.5 5.2 %collective-permute-start.1 = (bf16[64,512]{1,0:T(8,128)(2,1)S(1)}, bf16[64,512]{1,0:T(8,128)(2,1)S(1)}, u32[]{:S(2)}, u32[]{:S(2)}) collective-permute-start(bf16[64,512]{1,0:T(8,128)(2,1)S(1)} %get-tuple-element.13), channel_id=1, source_target_pairs={{0,8},{8,16},{16,24},{24,0},{1,9},{9,17},{17,25},{25,1},{2,10},{10... | collective-permute-start | bytes 196616 | tf_op jit(solution)/shard_map/ppermute | solution.py:534
  132.1 37.4 %all-to-all-start = ((bf16[8,128,512]{2,1,0:T(8,128)(2,1)}), bf16[8,128,512]{2,1,0:T(8,128)(2,1)S(1)}, u32[]{:S(2)}, u32[]{:S(2)}) async-start(bf16[8,128,512]{2,1,0:T(8,128)(2,1)} %bitcast.37), calls=%async_computation | async-start | bytes 2097152 | tf_op jit(solution)/shard_map/all_to_all | solution.py:651

commit v3 on v2

--- a/solution.py
+++ b/solution.py
@@ -16,17 +16,25 @@
 MIX_VMEM = 24 * 1024 * 1024
 PIECE = 16
 AHEAD = 2
-EXPERT_VMEM = 46 * 1024 * 1024
-
-
-def greet(axis):
+EXPERT_VMEM = 50 * 1024 * 1024
+
+
+def greet(axis, ring=None):
     n, me = lax.axis_size(axis), lax.axis_index(axis)
     barrier = pltpu.get_barrier_semaphore()
     for k in range(1, n):
         pl.semaphore_signal(
             barrier, inc=1, device_id={axis: lax.rem(me + k, n)}, device_id_type=MESH
         )
-    pl.semaphore_wait(barrier, n - 1)
+    count = n - 1
+    if ring is not None:
+        size, at = lax.axis_size(ring), lax.axis_index(ring)
+        for k in (1, size - 1):
+            pl.semaphore_signal(
+                barrier, inc=1, device_id={ring: lax.rem(at + k, size)}, device_id_type=MESH
+            )
+        count = count + 2
+    pl.semaphore_wait(barrier, count)
 
 
 def exchange_kernel(axis, parts, *refs):
@@ -358,7 +366,8 @@
 
 
 def expert_kernel(
-    axis, last, columns, picked_ref, gain_ref, router_ref, choice_ref, marks_ref, gate_hbm, up_hbm, down_hbm,
+    axis, ring, last, columns, picked_ref, gain_ref, router_ref, choice_ref, marks_ref, extra_ref, gate_hbm, up_hbm,
+    down_hbm,
     *refs,
 ):
     n, me = lax.axis_size(axis), lax.axis_index(axis)
@@ -367,14 +376,13 @@
     model, ff = gate_hbm.shape
     pieces = ff // columns
     if last:
-        o_ref, route_ref, full = refs[:3]
-        refs = refs[3:]
+        o_ref, route_ref, full, moved = refs[:4]
     else:
-        o_ref, full = refs[:2]
-        refs = refs[2:]
+        o_ref, full, arrived, arrived_ids = refs[:4]
+    refs = refs[4:]
     moe_in, hidden, gate, up, down, terms, held = refs[:7]
-    gate_sem, up_sem, down_sem, out_sem, in_sem = refs[7:12]
-    sems = refs[12:]
+    gate_sem, up_sem, down_sem, out_sem, in_sem, far_out, far_in, own_sem = refs[7:15]
+    sems = refs[15:]
 
     def fetch_in(hbm, buf, sem, i):
         at = pl.ds(pl.multiple_of(i * columns, columns), columns)
@@ -391,8 +399,35 @@
     for k in range(n):
         fetch_down(k if last else (k + 1) % n).start()
 
-    greet(axis)
-    spread(axis, picked_ref, column_block(width), full, *sems)
+    def far(device, source, target, k):
+        return pltpu.make_async_remote_copy(
+            src_ref=source,
+            dst_ref=target,
+            send_sem=far_out.at[k],
+            recv_sem=far_in.at[k],
+            device_id=device,
+            device_id_type=MESH,
+        )
+
+    sent = []
+    if last:
+        greet(axis)
+        spread(axis, picked_ref, column_block(width), full, *sems)
+        mine = column_block(width)(moved, me)
+        block_of = row_block(extra_ref.shape[0] // n)
+        for k in range(1, n):
+            peer = lax.rem(me + k, n)
+            sent.append(far({axis: peer}, block_of(extra_ref, peer), mine, k))
+        sent.append(pltpu.make_async_copy(block_of(extra_ref, me), mine, own_sem))
+        for copy in sent:
+            copy.start()
+    else:
+        greet(axis, ring)
+        size = lax.axis_size(ring)
+        following = {ring: lax.rem(lax.axis_index(ring) + 1, size)}
+        sent.append(far(following, extra_ref, arrived_ids, 0))
+        sent[0].start()
+        spread(axis, picked_ref, column_block(width), full, *sems)
 
     square = jnp.zeros((slots, 1), f32)
     for i in range(0, model, columns):
@@ -479,9 +514,13 @@
             total = total + held[k].astype(f32)
         expert_out = total.astype(bf16).astype(f32)
         o_ref[...] = (picked_ref[...].astype(f32) + weight * expert_out).astype(bf16)
-
-
-def expert(picked, gain, router, choice, marks, gate, up, down, last, axis, cid):
+        sent.append(far(following, o_ref, arrived, 1))
+        sent[1].start()
+    for copy in sent:
+        copy.wait()
+
+
+def expert(picked, gain, router, choice, marks, extra, gate, up, down, last, axis, ring, cid):
     n = lax.axis_size(axis)
     slots, width = picked.shape
     model, ff = gate.shape
@@ -494,13 +533,14 @@
     rows = jax.ShapeDtypeStruct(part, bf16)
     full = jax.ShapeDtypeStruct((slots, model), bf16)
     if last:
-        out_shape = [rows, jax.ShapeDtypeStruct((slots, 1), f32), full]
+        moved = jax.ShapeDtypeStruct((extra.shape[0] // n, model), bf16)
+        out_shape = [rows, jax.ShapeDtypeStruct((slots, 1), f32), full, moved]
     else:
-        out_shape = [rows, full]
+        out_shape = [rows, full, rows, jax.ShapeDtypeStruct(extra.shape, extra.dtype)]
     return pl.pallas_call(
-        functools.partial(expert_kernel, axis, last, columns),
+        functools.partial(expert_kernel, axis, ring, last, columns),
         out_shape=out_shape,
-        in_specs=[vmem] * 5 + [hbm] * 3,
+        in_specs=[vmem] * 6 + [hbm] * 3,
         out_specs=[vmem] * len(out_shape),
         scratch_shapes=[
             pltpu.VMEM((slots, model), bf16),
@@ -515,6 +555,9 @@
             dma((n,)),
             dma((2, n)),
             dma((2, n)),
+            dma((n,)),
+            dma((n,)),
+            dma,
         ]
         + spread_scratch(n),
         compiler_params=pltpu.CompilerParams(
@@ -526,7 +569,7 @@
             transcendentals=slots * ff,
         ),
         name=f"expert_{cid}",
-    )(picked, gain, router, choice, marks, gate, up, down)
+    )(picked, gain, router, choice, marks, extra, gate, up, down)
 
 
 def passed_along(x, axis):
@@ -646,12 +689,6 @@
         last = step + 1 == STEPS
         if not last:
             moved = passed_along(mixed, "section")
-            moved_ids = passed_along(all_ids[step], "section")
-        if last:
-            mixed = lax.all_to_all(
-                mixed.reshape(n, rows, width), "seq", split_axis=0, concat_axis=0
-            )
-            mixed = mixed.transpose(1, 0, 2).reshape(rows, model)
         slot_ids = jnp.dot(dispatch, all_ids[step].astype(bf16), preferred_element_type=f32)
         one_hot = (
             slot_ids[:, :, None] == jnp.arange(experts, dtype=jnp.int32).astype(f32)
@@ -666,15 +703,17 @@
             router[0].T,
             choice,
             marks,
+            mixed if last else all_ids[step].T,
             gate_weight[0],
             up_weight[0],
             down_weight[0],
             last,
             "seq",
+            "section",
             8 if last else 7,
         )
         if last:
-            expert_out, route, full = outs
+            expert_out, route, full, mixed = outs
             dispatch = lax.dynamic_slice(
                 dispatch, (me * capacity, me * rows), (capacity, rows)
             )
@@ -683,8 +722,8 @@
             picked = lax.dynamic_slice_in_dim(full, me * capacity, capacity, 0)
             new_rows = (picked.astype(f32) + route * expert_out.astype(f32)).astype(bf16)
         else:
-            new_rows = passed_along(outs[0], "section")
-            dispatch, routed = dispatch_of(moved_ids, n, capacity)
+            new_rows = outs[2]
+            dispatch, routed = dispatch_of(outs[3].T, n, capacity)
             mixed = moved
         placed = lax.dot_general(
             dispatch, new_rows, (((0,), (0,)), ((), ())), preferred_element_type=f32

time: 172 us -> 159 us (0.924)
  starting transfers between devices: 7.62 us -> 1.34 us
  waiting for transfers between devices: 4.02 us -> 0.01 us
  Pallas kernels: 141 us -> 139 us
    ppermute x3 -> x1, waiting for transfers between devices: 4.01 us -> 0.01 us  [passed_along(): return lax.ppermute(x, axis, [(i, (i + 1) % length) for i in range(length)])]
    all_to_all x1 -> x0, starting transfers between devices: 3.97 us -> none  [body(): lax.all_to_all(mixed.reshape(n, rows, width), 'seq', split_axis=0, concat...]
    ppermute x3 -> x1, starting transfers between devices: 3.65 us -> 1.34 us  [passed_along(): return lax.ppermute(x, axis, [(i, (i + 1) % length) for i in range(length)])]
  transfers between devices with their start and end apart: 4 -> 1, of which waited for: 1 -> 0; matrix products, arithmetic and copies ran while one was open for 2% -> 1% of each run, Pallas kernels for 33% -> 18%
where the time goes in v3:
time: 159 us; the launch traced here: 158 us
  Pallas kernels  139 us (87%)
  other arithmetic  6.68 us (4%)
  matrix products  6.66 us (4%)
  local copies, waits for them, and re-layouts  3.94 us (2%)
    pallas_call x2, Pallas kernels, mix(): pl.pallas_call(functools.partial(mixer_kernel, axis, nstate), out_shape=j...  62.7 us
    pallas_call x2, Pallas kernels, expert(): pl.pallas_call(functools.partial(expert_kernel, axis, ring, last, columns...  55.6 us
    pallas_call x2, Pallas kernels, exchange(): pl.pallas_call(functools.partial(exchange_kernel, axis, parts), out_shape...  21.1 us
    dot_general x2, matrix products, body(): lax.dot_general(dispatch, new_rows, (((0,), (0,)), ((), ())), preferred_e...  3.39 us
  transfers between devices with their start and end apart: 1, of which 0 were waited for; matrix products, arithmetic and copies ran while one was open for 1% of the time, Pallas kernels for 18%

profile of v3, /device:TPU:1, one launch (start us, length us, event | category | flops | bytes accessed | tf_op | source)
XLA Modules:
  0.0 158.3 jit_solution(995647462360579808)
XLA Ops:
  0.0 0.7 convert_element_type.155
  0.7 1.5 multiply_reduce_fusion
  2.2 0.0 copy-start
  2.2 1.2 copy-done
  3.4 16.7 %exchange_1.1 = (f32[8,8,128]{2,1,0:T(8,128)S(1)}, bf16[1024,512]{1,0:T(8,128)(2,1)S(1)}) custom-call(f32[8,128]{1,0:T(8,128)S(1)} %select_maximum_fusion.refs_0_, bf16[128,4096]{1,0:T(8,128)(2,1)S(1)} %bitcast.104), custom_call_target="tpu_custom_call" | custom-call | tf_op jit(solution)/shard_map/exchange_1/pallas_call | solution.py:71
  20.2 0.7 constant_dynamic-slice_fusion.5
  20.9 0.3 multiply_convert_fusion
  21.2 0.0 copy-start.4
  21.2 0.9 constant_dynamic-slice_fusion.2
  22.1 1.4 divide_multiply_fusion.1.x_ref
  23.5 0.0 copy-done.4
  23.5 0.0 copy-start.3
  23.5 0.5 convolution_convert_fusion.3.low_ref
  24.0 0.4 fusion.4.maps_ref
  24.4 0.8 multiply_bitcast_fusion.a_ref
  25.2 0.7 constant_dynamic-slice_fusion.3
  25.9 0.0 copy-done.3
  25.9 31.2 %mix_4.2 = bf16[1024,512]{1,0:T(8,128)(2,1)S(1)} custom-call(bf16[1024,256]{1,0:T(8,128)(2,1)S(1)} %convolution_convert_fusion.3.low_ref, bf16[32,1024]{1,0:T(8,128)(2,1)S(1)} %fusion.4.maps_ref, f32[1024,512]{1,0:T(8,128)S(1)} %divide_multiply_fusion.1.x_ref, bf16[1024,512]{1,0:T(8,128)(2,1)S(1)} %get-tuple-element.14.p_ref, ...), custom_call_target="tpu_custom_call" | custom-call | flops 50331648 | bytes 6291456 | tf_op jit(solution)/shard_map/mix_4/pallas_call | solution.py:330
  57.1 0.0 copy-start.1
  57.1 0.0 copy-start.2
  57.1 1.3 collective-permute-start
  58.5 0.2 fusion.10
  58.8 0.3 convolution_convert_fusion.6.picked_ref
  59.0 0.2 fusion.20
  59.2 0.2 fusion.9
  59.5 0.2 fusion.56
  59.7 0.1 compare_convert_fusion
  59.8 0.1 copy.30.marks_ref
  59.9 0.1 copy.31.marks_ref
  60.0 0.0 copy-done.1
  60.0 0.0 copy-done.2
  60.0 27.9 %expert_7.1 = (bf16[64,512]{1,0:T(8,128)(2,1)}, bf16[64,4096]{1,0:T(8,128)(2,1)}, bf16[64,512]{1,0:T(8,128)(2,1)S(1)}, f32[2,1024]{1,0:T(2,128)S(1)}) custom-call(bf16[64,512]{1,0:T(8,128)(2,1)S(1)} %convolution_convert_fusion.6.picked_ref, f32[1,4096]{1,0:T(1,128)S(1)} %copy-done.2, bf16[16,4096]{1,0:T(8,128)(2,1)S(1)} %bitcast.105, ...), custom_call_target="tpu_custom_call" | custom-call | flops 2415919104 | bytes 37748736 | tf_op jit(solution)/shard_map/expert_7/pallas_call | solution.py:540
  87.9 0.2 fusion.11
  88.1 0.1 fusion.18
  88.2 0.0 collective-permute-done
  88.2 1.9 %fusion = (f32[1024]{0:T(1024)S(1)}, bf16[1024,512]{1,0:T(8,128)(2,1)S(1)}) fusion(bf16[1024,512]{1,0:T(8,128)(2,1)} %collective-permute-done, bf16[64,512]{1,0:T(8,128)(2,1)S(1)} %get-tuple-element.16, s32[1024]{0:T(1024)S(1)} %fusion.11, pred[1024]{0:T(1024)(128)(4,1)S(1)} %or_reduce_fusion), kind=kOutput, calls=%fused_computation.3 | convolution fusion | flops 69860352 | bytes 2171904 | tf_op jit(solution)/shard_map/dot_general | solution.py:728
  90.1 4.4 %exchange_3.1 = f32[8,8,128]{2,1,0:T(8,128)S(1)} custom-call(f32[8,128]{1,0:T(8,128)S(1)} %bitcast.108), custom_call_target="tpu_custom_call" | custom-call | tf_op jit(solution)/shard_map/exchange_3/pallas_call | solution.py:71
  94.6 0.3 fusion.2
  94.9 1.4 divide_multiply_fusion.x_ref
  96.3 0.5 convolution_convert_fusion.2.low_ref
  96.8 0.4 fusion.5.maps_ref
  97.2 31.5 %mix_4.3.extra_ref = bf16[1024,512]{1,0:T(8,128)(2,1)S(1)} custom-call(bf16[1024,256]{1,0:T(8,128)(2,1)S(1)} %convolution_convert_fusion.2.low_ref, bf16[32,1024]{1,0:T(8,128)(2,1)S(1)} %fusion.5.maps_ref, f32[1024,512]{1,0:T(8,128)S(1)} %divide_multiply_fusion.x_ref, bf16[1024,512]{1,0:T(8,128)(2,1)S(1)} %get-tuple-element.38.p_ref, ...), custom_call_target="tpu_custom_call" | custom-call | flops 50331648 | bytes 6291456 | tf_op jit(solution)/shard_map/mix_4/pallas_call | solution.py:330
  128.7 0.3 convolution_convert_fusion.4.picked_ref
  128.9 27.7 %expert_8.1 = (bf16[8,4096]{1,0:T(8,128)(2,1)S(1)}, f32[64,1]{1,0:T(8,128)S(1)}, bf16[64,4096]{1,0:T(8,128)(2,1)S(1)}, bf16[128,4096]{1,0:T(8,128)(2,1)S(1)}) custom-call(bf16[64,512]{1,0:T(8,128)(2,1)S(1)} %convolution_convert_fusion.4.picked_ref, f32[1,4096]{1,0:T(1,128)S(1)} %copy-done.2, bf16[16,4096]{1,0:T(8,128)(2,1)S(1)} %bitcast.106, ...), custom_call_target="tpu_custom_call" | custom-call | flops 2415919104 | bytes 37748736 | tf_op jit(solution)/shard_map/expert_8/pallas_call | solution.py:540
  156.7 0.1 dynamic-slice_reduce_fusion
  156.8 1.5 select_bitcast_fusion
  (20 shorter events, 0.2 us)
Async XLA Ops:
  2.2 1.2 copy-start
  21.2 2.3 %copy-start.4 = (bf16[1,512,288]{1,2,0:T(8,128)(2,1)S(1)}, bf16[1,512,288]{1,2,0:T(8,128)(2,1)}, u32[]{:S(2)}) copy-start(bf16[1,512,288]{1,2,0:T(8,128)(2,1)} %param.19) | copy-start | bytes 884740
  23.5 2.4 %copy-start.3 = (bf16[1,256,512]{2,1,0:T(8,128)(2,1)S(1)}, bf16[1,256,512]{2,1,0:T(8,128)(2,1)}, u32[]{:S(2)}) copy-start(bf16[1,256,512]{2,1,0:T(8,128)(2,1)} %param.20) | copy-start | bytes 786436
  57.1 2.9 %copy-start.1 = (bf16[1,4096,16]{1,2,0:T(8,128)(2,1)S(1)}, bf16[1,4096,16]{1,2,0:T(8,128)(2,1)}, u32[]{:S(2)}) copy-start(bf16[1,4096,16]{1,2,0:T(8,128)(2,1)} %param.25) | copy-start | bytes 393220
  57.1 2.9 %copy-start.2 = (f32[1,4096]{1,0:T(1,128)S(1)}, f32[1,4096]{1,0:T(1,128)}, u32[]{:S(2)}) copy-start(f32[1,4096]{1,0:T(1,128)} %gain_ref.3) | copy-start | bytes 49156
  57.1 31.1 %collective-permute-start = (bf16[1024,512]{1,0:T(8,128)(2,1)S(1)}, bf16[1024,512]{1,0:T(8,128)(2,1)}, u32[]{:S(2)}, u32[]{:S(2)}) collective-permute-start(bf16[1024,512]{1,0:T(8,128)(2,1)S(1)} %mix_4.2), channel_id=1, source_target_pairs={{0,8},{8,16},{16,24},{24,0},{1,9},{9,17},{17,25},{25,1},{2,10},{10... | collective-permute-start | bytes 3145736 | tf_op jit(solution)/shard_map/ppermute | solution.py:577
